TPU v7x, 128 devices: a whole 4x4x4 slice. The times are simulated.
128 devices in a mesh: gx: 16 (over z, y_hi, core), gy: 8 (over x, y_lo).
Axes of the slice: x: 4, y: 4 (y_hi: 2, y_lo: 2; y = y_hi * 2 + y_lo), z: 4, core: 2. Of those that a mesh axis runs over, the one named last changes fastest.
Arguments:
- density: float32 [512, 2048], P('gx', 'gy'), may hold values from 0.5 to 2
- momentum: float32 [3, 512, 2048], P(None, 'gx', 'gy'), may hold values from -0.6 to 0.6
- magnetic: float32 [3, 512, 2048], P(None, 'gx', 'gy'), may hold values from -0.6 to 0.6
- shear_shift: int32 [8], replicated, may hold values from 0 to 2047
- shear_frac: float32 [8], replicated, may hold values from 0 to 1
Outputs:
- density_next: float32 [512, 2048], P('gx', 'gy')
- momentum_next: float32 [3, 512, 2048], P(None, 'gx', 'gy')
- magnetic_next: float32 [3, 512, 2048], P(None, 'gx', 'gy')
All inputs are finite; a program needn't handle non-finite values.
Results may differ from a plain program's by a relative error of at most 0.0003.
Values sent between devices are 32-bit elements; how exact they have to be, the bound alone decides.
A program may use at most 128 MiB of HBM per device.

v0:
```python
import functools

import jax
import jax.numpy as jnp
from jax import lax
from jax.experimental import pallas as pl
from jax.experimental.pallas import tpu as pltpu
from jax.sharding import PartitionSpec as P

STEPS = 8
OMEGA = 0.5
QSHEAR = 1.5
TIMESTEP = 0.1
MESH = pl.DeviceIdType.MESH

D, MX, MY, MZ, BZ, BX, BY = range(7)
VX, VY, VZ, CY, CX, QBZ = 1, 2, 3, 4, 5, 6
OWN = 4
GHOST = OWN
STRIP = OWN + 1
TILES = OWN + 2
LANES = 384


def roll(x, shift, axis):
    return pltpu.roll(x, shift % x.shape[axis], axis)


def row_iota(shape):
    return lax.broadcasted_iota(jnp.int32, shape, len(shape) - 2)


def lane_iota(shape):
    return lax.broadcasted_iota(jnp.int32, shape, len(shape) - 1)


def kernel(
    gxn, gyn, shift_ref, frac_ref, den, mom, mag, den_out, mom_out, mag_out,
    U, Q, M, QL, QR, FX, PART, FY4, SX4, EZ, NBX, NBY,
    pack_lo, pack_hi, recv_lo, recv_hi, circ, ring, far, col_r, col_l,
    col_send, col_recv, row_send, row_recv, circ_send, circ_recv,
):
    gx = lax.axis_index("gx")
    gy = lax.axis_index("gy")
    at_low = gx == 0
    at_high = gx == gxn - 1
    at_end = jnp.logical_or(at_low, at_high)
    not_low = gx > 0
    not_high = gx < gxn - 1
    east = lax.rem(gy + 1, gyn)
    west = lax.rem(gy + gyn - 1, gyn)
    circle = 2 * gyn

    rows8 = row_iota((8, LANES))
    lanes8 = lane_iota((8, LANES))
    first_row = rows8 == 0
    last_row = rows8 == 7

    def previous(k):
        return STRIP if k == STRIP else (k + STRIP - 1) % STRIP

    def following(k):
        return STRIP if k == STRIP else (k + 1) % STRIP

    def row_before(before, here):
        return roll(jnp.where(last_row, before, here), 1, 0)

    def row_after(here, after):
        return roll(jnp.where(first_row, after, here), -1, 0)

    def lane_before(x):
        return roll(x, 1, 1)

    def lane_after(x):
        return roll(x, -1, 1)

    barrier = pltpu.get_barrier_semaphore()
    for partner in (east, west):
        pl.semaphore_signal(barrier, inc=1, device_id=(gx, partner), device_id_type=MESH)

    @pl.when(not_low)
    def _():
        pl.semaphore_signal(barrier, inc=1, device_id=(gx - 1, gy), device_id_type=MESH)

    @pl.when(not_high)
    def _():
        pl.semaphore_signal(barrier, inc=1, device_id=(gx + 1, gy), device_id_type=MESH)

    @pl.when(at_end)
    def _():
        other = gxn - 1 - gx
        for g in range(gyn):
            pl.semaphore_signal(barrier, inc=1, device_id=(other, g), device_id_type=MESH)

    def source_rows(field, k):
        rows = pl.ds(8 * k, 8)
        if field == D:
            return den[rows, :]
        if field in (MX, MY, MZ):
            return mom[field - MX, rows, :]
        return mag[{BX: 0, BY: 1, BZ: 2}[field], rows, :]

    for field in range(7):
        for k in range(OWN):
            U[field, k, :, 0:256] = source_rows(field, k)

    pl.semaphore_wait(barrier, jnp.where(at_end, 3 + gyn, 4))

    to_west = pltpu.make_async_remote_copy(
        src_ref=U.at[:, 0:OWN, :, 0:128], dst_ref=col_r, send_sem=col_send.at[0], recv_sem=col_recv.at[0],
        device_id=(gx, west), device_id_type=MESH,
    )
    to_east = pltpu.make_async_remote_copy(
        src_ref=U.at[:, 0:OWN, :, 128:256], dst_ref=col_l, send_sem=col_send.at[1], recv_sem=col_recv.at[1],
        device_id=(gx, east), device_id_type=MESH,
    )
    to_west.start()
    to_east.start()
    to_west.wait()
    to_east.wait()
    near = lane_iota((8, 128)) < 64
    for field in range(7):
        for k in range(OWN):
            U[field, k, :, 256:384] = jnp.where(near, col_r[field, k], col_l[field, k])
        for k in (GHOST, STRIP):
            U[field, k] = U[field, 0]

    def packed(tiles, first):
        def at(field, row):
            return tiles[field] if row == first else roll(tiles[field], row - first, 0)

        return (
            jnp.where(rows8 < 3, at(0, 0), jnp.where(rows8 < 6, at(1, 3), at(6, 6))),
            jnp.where(rows8 < 3, at(2, 0), jnp.where(rows8 < 6, at(3, 3), at(6, 4))),
            jnp.where(rows8 < 3, at(4, 0), at(5, 3)),
        )

    def unpacked(tiles, first):
        def move(x, row):
            return x if row == first else roll(x, first - row, 0)

        sixth = jnp.where(rows8 < first + 2, move(tiles[0], 6), move(tiles[1], 4))
        return (
            move(tiles[0], 0), move(tiles[0], 3), move(tiles[1], 0), move(tiles[1], 3),
            move(tiles[2], 0), move(tiles[2], 3), sixth,
        )

    def store_pack(ref, slot, tiles):
        for part in range(3):
            for lane in range(3):
                ref[slot, lane, part] = tiles[part][:, 128 * lane : 128 * (lane + 1)]

    def load_pack(ref, slot):
        return [jnp.concatenate([ref[slot, lane, part] for lane in range(3)], axis=1) for part in range(3)]

    ghost_above = rows8 < 3
    ghost_below = rows8 >= 5

    def minmod(a, b):
        return jnp.maximum(jnp.minimum(a, b), 0.0) + jnp.minimum(jnp.maximum(a, b), 0.0)

    def signal(density, speed, squared):
        total = density + squared
        return jnp.abs(speed) + jnp.abs(total) * lax.rsqrt(total * density)

    def riemann(left, right, normal, wanted):
        dl, vnl, vtl, vsl, btl, bsl = left
        dr, vnr, vtr, vsr, btr, bsr = right
        n2 = normal * normal
        tl = btl * btl + bsl * bsl
        tr = btr * btr + bsr * bsr
        fastest = jnp.maximum(signal(dl, vnl, n2 + tl), signal(dr, vnr, n2 + tr))
        out = {}
        if 0 in wanted or 1 in wanted or 2 in wanted or 3 in wanted:
            ml = dl * vnl
            mr = dr * vnr
        if 0 in wanted:
            out[0] = ml + mr - fastest * (dr - dl)
        if 1 in wanted:
            out[1] = (ml * vnl + mr * vnr) + (dl + dr) + 0.5 * (tl + tr) - n2 - fastest * (mr - ml)
        if 2 in wanted:
            out[2] = (ml * vtl + mr * vtr) - normal * (btl + btr) - fastest * (dr * vtr - dl * vtl)
        if 3 in wanted:
            out[3] = (ml * vsl + mr * vsr) - normal * (bsl + bsr) - fastest * (dr * vsr - dl * vsl)
        if 4 in wanted:
            out[4] = (btl * vnl + btr * vnr) - normal * (vtl + vtr) - fastest * (btr - btl)
        if 5 in wanted:
            out[5] = (bsl * vnl + bsr * vnr) - normal * (vsl + vsr) - fastest * (bsr - bsl)
        return out

    def primitives(k, density, mx, my, mz, bz, bx, bx_after, by):
        inverse = 1.0 / density
        Q[0, k] = density
        Q[VX, k] = mx * inverse
        Q[VY, k] = my * inverse
        Q[VZ, k] = mz * inverse
        Q[CX, k] = 0.5 * (bx + row_after(bx, bx_after))
        Q[CY, k] = 0.5 * (by + lane_after(by))
        Q[QBZ, k] = bz

    def initial_primitives(k):
        primitives(k, *(U[f, k] for f in (D, MX, MY, MZ, BZ, BX)), U[BX, following(k)], U[BY, k])

    X_STATE = (0, VX, VY, VZ, CY, QBZ)
    Y_STATE = (0, VY, VX, VZ, CX, QBZ)

    def finish_fluxes(k, fx, fy, stride, mx, my, cells):
        half = 0.5 * stride
        if 0 in fx:
            for spot, part in enumerate((0, 1, 2, 3, 5)):
                FX[spot, k] = fx[part]
        FY4[k] = fy[4]
        SX4[k] = fx[4] + lane_before(fx[4])
        if cells:
            for spot, (field, px, py) in enumerate(((D, 0, 0), (MX, 1, 2), (MY, 2, 1), (MZ, 3, 3), (BZ, 5, 5))):
                value = U[field, k] - half * ((lane_after(fy[py]) - fy[py]) - fx[px])
                if field == MX:
                    value += (stride * 2.0 * OMEGA) * my
                if field == MY:
                    value -= (stride * (2.0 - QSHEAR) * OMEGA) * mx
                PART[spot, k] = value

    ALL = (0, 1, 2, 3, 4, 5)

    def first_order(k, stride):
        left = [row_before(Q[i, previous(k)], Q[i, k]) for i in X_STATE]
        fx = riemann(left, [Q[i, k] for i in X_STATE], U[BX, k], ALL)
        right = [Q[i, k] for i in Y_STATE]
        fy = riemann([lane_before(q) for q in right], right, U[BY, k], ALL)
        finish_fluxes(k, fx, fy, stride, U[MX, k], U[MY, k], True)

    def slopes(k):
        for spot, i in enumerate(X_STATE):
            here = Q[i, k]
            gradient = 0.5 * minmod(here - row_before(Q[i, previous(k)], here), row_after(here, Q[i, following(k)]) - here)
            QL[spot, k] = here + gradient
            QR[spot, k] = here - gradient

    def second_order(k, stride):
        cells = k < OWN
        x_wanted = ALL if k < STRIP else (4,)
        y_wanted = ALL if cells else (4,)
        left = [row_before(QL[i, previous(k)], QL[i, k]) for i in range(6)]
        fx = riemann(left, [QR[i, k] for i in range(6)], NBX[k], x_wanted)
        left, right = [], []
        for i in Y_STATE:
            here = Q[i, k]
            behind = here - lane_before(here)
            gradient = 0.5 * minmod(behind, lane_after(behind))
            left.append(lane_before(here + gradient))
            right.append(here - gradient)
        fy = riemann(left, right, NBY[k], y_wanted)
        finish_fluxes(k, fx, fy, stride, M[0, k], M[1, k], cells)

    def corner(k):
        return 0.125 * (FY4[k] + row_before(FY4[previous(k)], FY4[k]) - SX4[k])

    def face_x(k, emf, stride):
        EZ[k] = emf
        return U[BX, k] - stride * (lane_after(emf) - emf)

    def face_y(k, stride):
        emf = EZ[k]
        return U[BY, k] + stride * (row_after(emf, EZ[following(k)]) - emf)

    def cells_of(k, stride):
        return [PART[i, k] - (0.5 * stride) * row_after(FX[i, k], FX[i, following(k)]) for i in range(5)]

    def tiles(run, *ends):
        for k in range(STRIP):
            run(k)
        if ends:

            @pl.when(at_end)
            def _():
                run(STRIP)

    def step(n, carry):
        slot = lax.rem(n, 2)
        fraction = frac_ref[n]
        shift = shift_ref[n]

        store_pack(pack_lo, slot, packed([U[f, 0] for f in range(7)], 0))
        store_pack(pack_hi, slot, packed([U[f, OWN - 1] for f in range(7)], 5))

        def to_far(pack, g):
            return pltpu.make_async_remote_copy(
                src_ref=pack.at[slot, 0:2], dst_ref=circ.at[slot, pl.ds(2 * gy, 2)],
                send_sem=circ_send.at[g], recv_sem=circ_recv.at[slot, gy],
                device_id=(gxn - 1 - gx, g), device_id_type=MESH,
            )

        def from_far(g):
            return pltpu.make_async_remote_copy(
                src_ref=pack_lo.at[slot, 0:2], dst_ref=circ.at[slot, pl.ds(2 * g, 2)],
                send_sem=circ_send.at[g], recv_sem=circ_recv.at[slot, g],
                device_id=(gxn - 1 - gx, g), device_id_type=MESH,
            )

        down = pltpu.make_async_remote_copy(
            src_ref=pack_lo.at[slot], dst_ref=recv_hi.at[slot], send_sem=row_send.at[0], recv_sem=row_recv.at[slot, 0],
            device_id=(lax.max(gx - 1, 0), gy), device_id_type=MESH,
        )
        up = pltpu.make_async_remote_copy(
            src_ref=pack_hi.at[slot], dst_ref=recv_lo.at[slot], send_sem=row_send.at[1], recv_sem=row_recv.at[slot, 1],
            device_id=(lax.min(gx + 1, gxn - 1), gy), device_id_type=MESH,
        )

        @pl.when(at_low)
        def _():
            for g in range(gyn):
                to_far(pack_lo, g).start()

        @pl.when(at_high)
        def _():
            for g in range(gyn):
                to_far(pack_hi, g).start()

        @pl.when(not_low)
        def _():
            down.start()

        @pl.when(not_high)
        def _():
            up.start()

        @pl.when(not_high)
        def _():
            down.wait_recv()
            for f, tile in enumerate(unpacked(load_pack(recv_hi, slot), 0)):
                U[f, GHOST] = jnp.where(ghost_above, tile, U[f, GHOST])

        @pl.when(not_low)
        def _():
            up.wait_recv()
            for f, tile in enumerate(unpacked(load_pack(recv_lo, slot), 5)):
                U[f, GHOST] = jnp.where(ghost_below, tile, U[f, GHOST])

        @pl.when(at_end)
        def _():
            for g in range(gyn):
                from_far(g).wait_recv()
            for place in range(circle):
                for part in range(3):
                    ring[place, part] = circ[slot, place, part]
            moved = jnp.where(at_low, -shift, shift)
            origin = lax.rem(gy * 256 + moved + 256 * gyn, 256 * gyn)
            lane_tile = lax.div(origin, 128)
            offset = lax.rem(origin, 128)
            turn = lax.rem(128 - offset, 128)
            inside = lane_iota((8, 128)) < 128 - offset
            for part in range(3):
                turned = []
                for i in range(5):
                    place = lax.rem(lane_tile + (circle - 1 + i), circle)
                    turned.append(pltpu.roll(ring[place, part], turn, 1))
                spans = [jnp.where(inside, a, b) for a, b in zip(turned[:-1], turned[1:])]
                far[part, :, 0:128] = spans[1]
                far[part, :, 128:256] = spans[2]
                far[part, :, 256:384] = jnp.where(near, spans[3], spans[0])

        def blended(x, towards):
            return (1.0 - fraction) * x + fraction * roll(x, -towards, 1)

        @pl.when(at_low)
        def _():
            raw = [far[part] for part in range(3)]
            for f, tile in enumerate(unpacked([blended(x, -1) for x in raw], 5)):
                U[f, GHOST] = jnp.where(ghost_below, tile, U[f, GHOST])
            for f, tile in enumerate(unpacked(raw, 0)):
                own = roll(blended(U[f, 0], 1), 3, 0)
                U[f, STRIP] = jnp.where(ghost_above, tile, own)

        @pl.when(at_high)
        def _():
            raw = [far[part] for part in range(3)]
            for f, tile in enumerate(unpacked([blended(x, 1) for x in raw], 0)):
                U[f, GHOST] = jnp.where(ghost_above, tile, U[f, GHOST])
            for f, tile in enumerate(unpacked(raw, 3)):
                own = roll(blended(U[f, OWN - 1], -1), 3, 0)
                U[f, STRIP] = jnp.where(ghost_above, own, tile)

        stride = 0.5 * TIMESTEP
        tiles(initial_primitives, True)
        tiles(lambda k: first_order(k, stride), True)

        def predicted_x(k):
            NBX[k] = face_x(k, corner(k), stride)

        tiles(predicted_x, True)

        def predicted_cells(k):
            density, mx, my, mz, bz = cells_of(k, stride)
            by = face_y(k, stride)
            NBY[k] = by
            M[0, k] = mx
            M[1, k] = my
            primitives(k, density, mx, my, mz, bz, NBX[k], NBX[following(k)], by)

        tiles(predicted_cells, True)

        tiles(slopes, True)
        tiles(lambda k: second_order(k, TIMESTEP), True)

        @pl.when(at_end)
        def _():
            EZ[STRIP] = corner(STRIP)

        emf_strip = EZ[STRIP]
        towards = jnp.where(at_low, lane_before(emf_strip), lane_after(emf_strip))
        remote = (1.0 - fraction) * emf_strip + fraction * towards
        remote = roll(remote, -3, 0)
        for k in range(STRIP):
            emf = corner(k)
            if k in (0, GHOST):
                ours = at_low if k == 0 else at_high
                fixed = jnp.where(first_row, 0.5 * (emf + remote), emf)
                emf = jnp.where(ours, fixed, emf)
            new_bx = face_x(k, emf, TIMESTEP)
            if k < OWN:
                U[BX, k] = new_bx
        for k in range(OWN):
            for field, value in zip((D, MX, MY, MZ, BZ), cells_of(k, TIMESTEP)):
                U[field, k] = value
            U[BY, k] = face_y(k, TIMESTEP)

        @pl.when(at_low)
        def _():
            for g in range(gyn):
                to_far(pack_lo, g).wait_send()

        @pl.when(at_high)
        def _():
            for g in range(gyn):
                to_far(pack_hi, g).wait_send()

        @pl.when(not_low)
        def _():
            down.wait_send()

        @pl.when(not_high)
        def _():
            up.wait_send()

        return carry

    EZ[STRIP] = jnp.zeros((8, LANES), jnp.float32)
    lax.fori_loop(0, STEPS, step, 0)

    for k in range(OWN):
        rows = pl.ds(8 * k, 8)
        den_out[rows, :] = U[D, k, :, 0:256]
        for i, field in enumerate((MX, MY, MZ)):
            mom_out[i, rows, :] = U[field, k, :, 0:256]
        for i, field in enumerate((BX, BY, BZ)):
            mag_out[i, rows, :] = U[field, k, :, 0:256]


def scratch(gyn):
    tile = (TILES, 8, LANES)
    f32 = jnp.float32
    vmem = lambda *shape: pltpu.VMEM(shape, f32)
    dma = pltpu.SemaphoreType.DMA
    return [
        vmem(7, *tile), vmem(7, *tile), vmem(2, *tile), vmem(6, *tile), vmem(6, *tile), vmem(5, *tile), vmem(5, *tile),
        vmem(*tile), vmem(*tile), vmem(*tile), vmem(*tile), vmem(*tile),
        vmem(2, 3, 3, 8, 128), vmem(2, 3, 3, 8, 128), vmem(2, 3, 3, 8, 128), vmem(2, 3, 3, 8, 128),
        vmem(2, 2 * gyn, 3, 8, 128), vmem(2 * gyn, 3, 8, 128), vmem(3, 8, LANES), vmem(7, OWN, 8, 128), vmem(7, OWN, 8, 128),
        dma((2,)), dma((2,)), dma((2,)), dma((2, 2)), dma((gyn,)), dma((2, gyn)),
    ]


def solution(mesh):
    gxn, gyn = mesh.shape["gx"], mesh.shape["gy"]

    def per_device(density, momentum, magnetic, shear_shift, shear_frac):
        return pl.pallas_call(
            functools.partial(kernel, gxn, gyn),
            name="shearing_box",
            out_shape=tuple(jax.ShapeDtypeStruct(a.shape, jnp.float32) for a in (density, momentum, magnetic)),
            in_specs=[pl.BlockSpec(memory_space=pltpu.SMEM)] * 2 + [pl.BlockSpec(memory_space=pltpu.VMEM)] * 3,
            out_specs=tuple(pl.BlockSpec(memory_space=pltpu.VMEM) for _ in range(3)),
            scratch_shapes=scratch(gyn),
            compiler_params=pltpu.CompilerParams(
                collective_id=0, has_side_effects=True, vmem_limit_bytes=32 * 1024 * 1024
            ),
        )(shear_shift, shear_frac, density, momentum, magnetic)

    return jax.shard_map(
        per_device,
        mesh=mesh,
        in_specs=(P("gx", "gy"), P(None, "gx", "gy"), P(None, "gx", "gy"), P(), P()),
        out_specs=(P("gx", "gy"), P(None, "gx", "gy"), P(None, "gx", "gy")),
        check_vma=False,
    )
```

profile of v0, /device:TPU:0, one launch (start us, length us, event | category | flops | bytes accessed | tf_op | source)
XLA Modules:
  0.0 95.3 jit_solution(3609014905928003665)
XLA Ops:
  0.6 0.0 copy-start
  0.6 0.9 copy-done
  1.5 0.0 copy-start.1
  1.5 0.9 copy-done.1
  2.4 0.0 copy-start.2
  2.4 0.8 copy-done.2
  3.2 0.0 copy-start.3
  3.2 0.7 copy-done.3
  3.8 0.0 copy-start.4
  3.8 0.7 copy-done.4
  4.5 88.9 %shearing_box.1 = (f32[32,256]{1,0:T(8,128)S(1)}, f32[3,32,256]{2,1,0:T(8,128)S(1)}, f32[3,32,256]{2,1,0:T(8,128)S(1)}) custom-call(s32[8]{0:T(128)S(1)} %copy-done.3, f32[8]{0:T(128)S(1)} %copy-done.4, f32[32,256]{1,0:T(8,128)S(1)} %copy-done.2, f32[3,32,256]{2,1,0:T(8,128)S(1)} %copy-done, f32[3,32,256]{2,1,0:T(8,128)S(1)} %copy-done.1), custom_call_target="tpu_custom_call" | custom-call | tf_op jit(solution)/shard_map/shearing_box/pallas_call | solution.py:477
  93.4 0.6 copy.11
  94.1 0.6 copy.12
  94.7 0.6 copy.13
Async XLA Ops:
  0.6 0.9 copy-start
  1.5 0.9 copy-start.1
  2.4 0.8 copy-start.2
  3.2 0.7 copy-start.3
  3.8 0.7 copy-start.4
where the time goes:
time: 95.6 us; the launch traced here: 95.3 us
  Pallas kernels  88.9 us (93%)
  local copies, waits for them, and re-layouts  5.74 us (6%)
    pallas_call x1, Pallas kernels, per_device(): pl.pallas_call(functools.partial(kernel, gxn, gyn), name='shearing_box',...  88.9 us
    unnamed x13, local copies, waits for them, and re-layouts  5.74 us

commit v1 on v0

v1 whole, which is shorter than its diff:
```python
import functools

import jax
import jax.numpy as jnp
from jax import lax
from jax.experimental import pallas as pl
from jax.experimental.pallas import tpu as pltpu
from jax.sharding import PartitionSpec as P

STEPS = 8
OMEGA = 0.5
QSHEAR = 1.5
TIMESTEP = 0.1
MESH = pl.DeviceIdType.MESH

D, MX, MY, MZ, BX, BY, BZ = range(7)
VX, VY, VZ, CY, CX, QBZ = 1, 2, 3, 4, 5, 6
OWN = 4
ABOVE, BELOW = OWN, OWN + 1
RING = OWN + 2
AHEAD = (RING, RING + 1)
TILES = RING + 2
LANES = 384
PARTS = 6


def roll(x, shift, axis):
    return pltpu.roll(x, shift % x.shape[axis], axis)


def row_iota(shape):
    return lax.broadcasted_iota(jnp.int32, shape, len(shape) - 2)


def lane_iota(shape):
    return lax.broadcasted_iota(jnp.int32, shape, len(shape) - 1)


def kernel(
    gxn, gyn, shift_in, frac_in, den, mom, mag, den_out, mom_out, mag_out,
    U, Q, M, QL, QR, FX, PART, FY4, SX4, EZ, NBX, NBY,
    pack_lo, pack_hi, recv_lo, recv_hi, diagonal, circ_far, circ_near, ring_far, ring_near, col_r, col_l,
    shift_ref, frac_ref, load_sem,
    col_send, col_recv, row_send, row_recv, dia_send, dia_recv, far_send, far_recv, near_send, near_recv,
):
    gx = lax.axis_index("gx")
    gy = lax.axis_index("gy")
    at_low = gx == 0
    at_high = gx == gxn - 1
    at_end = jnp.logical_or(at_low, at_high)
    not_low = gx > 0
    not_high = gx < gxn - 1
    below_gx = lax.max(gx - 1, 0)
    above_gx = lax.min(gx + 1, gxn - 1)
    other_end = gxn - 1 - gx
    east = lax.rem(gy + 1, gyn)
    west = lax.rem(gy + gyn - 1, gyn)
    circle = 2 * gyn

    rows8 = row_iota((8, LANES))
    first_row = rows8 == 0
    last_row = rows8 == 7
    near = lane_iota((8, 128)) < 64

    def previous(k):
        return sum(AHEAD) - k if k in AHEAD else (k + RING - 1) % RING

    def following(k):
        return sum(AHEAD) - k if k in AHEAD else (k + 1) % RING

    def row_before(before, here):
        return roll(jnp.where(last_row, before, here), 1, 0)

    def row_after(here, after):
        return roll(jnp.where(first_row, after, here), -1, 0)

    def lane_before(x):
        return roll(x, 1, 1)

    def lane_after(x):
        return roll(x, -1, 1)

    loads = [
        pltpu.make_async_copy(den, U.at[D, 0:OWN, :, 0:256], load_sem.at[0]),
        pltpu.make_async_copy(mom, U.at[MX : MZ + 1, 0:OWN, :, 0:256], load_sem.at[1]),
        pltpu.make_async_copy(mag, U.at[BX : BZ + 1, 0:OWN, :, 0:256], load_sem.at[2]),
        pltpu.make_async_copy(shift_in, shift_ref, load_sem.at[3]),
        pltpu.make_async_copy(frac_in, frac_ref, load_sem.at[4]),
    ]
    for load in loads:
        load.start()

    barrier = pltpu.get_barrier_semaphore()

    def greet(to_gx, to_gy):
        pl.semaphore_signal(barrier, inc=1, device_id=(to_gx, to_gy), device_id_type=MESH)

    @pl.when(at_end)
    def _():
        for g in range(gyn):
            greet(other_end, g)
        for i in range(1, gyn):
            greet(gx, lax.rem(gy + i, gyn))

    @pl.when(jnp.logical_not(at_end))
    def _():
        greet(gx, east)
        greet(gx, west)

    @pl.when(not_low)
    def _():
        for g in (west, gy, east):
            greet(below_gx, g)

    @pl.when(not_high)
    def _():
        for g in (west, gy, east):
            greet(above_gx, g)

    for load in loads:
        load.wait()

    def packed(tiles, first):
        def at(field, row):
            return tiles[field] if row == first else roll(tiles[field], row - first, 0)

        return [
            jnp.where(rows8 < 3, at(0, 0), jnp.where(rows8 < 6, at(1, 3), at(6, 6))),
            jnp.where(rows8 < 3, at(2, 0), jnp.where(rows8 < 6, at(3, 3), at(6, 4))),
            jnp.where(rows8 < 3, at(4, 0), at(5, 3)),
        ]

    def unpacked(tiles, first):
        def move(x, row):
            return x if row == first else roll(x, first - row, 0)

        sixth = jnp.where(((rows8 - first) & 7) < 2, move(tiles[0], 6), move(tiles[1], 4))
        return (
            move(tiles[0], 0), move(tiles[0], 3), move(tiles[1], 0), move(tiles[1], 3),
            move(tiles[2], 0), move(tiles[2], 3), sixth,
        )

    def pack_edge(ref, slot, k, outer, inner):
        tiles = [U[f, k] for f in range(7)]
        for part, tile in enumerate(packed(tiles, outer) + packed(tiles, inner)):
            for lane in range(3):
                ref[slot, lane, part] = tile[:, 128 * lane : 128 * (lane + 1)]

    def load_pack(ref, slot, parts):
        return [jnp.concatenate([ref[slot, lane, part] for lane in range(3)], axis=1) for part in parts]

    def pack_edges(slot):
        pack_edge(pack_lo, slot, 0, 0, 3)
        pack_edge(pack_hi, slot, OWN - 1, 5, 2)

    def to_far(pack, slot, g):
        return pltpu.make_async_remote_copy(
            src_ref=pack.at[slot, 0:2], dst_ref=circ_far.at[slot, pl.ds(2 * gy, 2)],
            send_sem=far_send.at[g], recv_sem=far_recv.at[slot, gy],
            device_id=(other_end, g), device_id_type=MESH,
        )

    def from_far(slot, g):
        return pltpu.make_async_remote_copy(
            src_ref=pack_lo.at[slot, 0:2], dst_ref=circ_far.at[slot, pl.ds(2 * g, 2)],
            send_sem=far_send.at[g], recv_sem=far_recv.at[slot, g],
            device_id=(other_end, g), device_id_type=MESH,
        )

    def to_near(pack, slot, i):
        return pltpu.make_async_remote_copy(
            src_ref=pack.at[slot, 0:2, 0:3], dst_ref=circ_near.at[slot, pl.ds(2 * gy, 2)],
            send_sem=near_send.at[i], recv_sem=near_recv.at[slot, i],
            device_id=(gx, lax.rem(gy + i, gyn)), device_id_type=MESH,
        )

    def from_near(slot, i):
        sender = lax.rem(gy + gyn - i, gyn)
        return pltpu.make_async_remote_copy(
            src_ref=pack_lo.at[slot, 0:2, 0:3], dst_ref=circ_near.at[slot, pl.ds(2 * sender, 2)],
            send_sem=near_send.at[i], recv_sem=near_recv.at[slot, i],
            device_id=(gx, sender), device_id_type=MESH,
        )

    def down(slot):
        return pltpu.make_async_remote_copy(
            src_ref=pack_lo.at[slot], dst_ref=recv_hi.at[slot], send_sem=row_send.at[0], recv_sem=row_recv.at[slot, 0],
            device_id=(below_gx, gy), device_id_type=MESH,
        )

    def up(slot):
        return pltpu.make_async_remote_copy(
            src_ref=pack_hi.at[slot], dst_ref=recv_lo.at[slot], send_sem=row_send.at[1], recv_sem=row_recv.at[slot, 1],
            device_id=(above_gx, gy), device_id_type=MESH,
        )

    def diagonals(pack, side, to_gx):
        return [
            pltpu.make_async_remote_copy(
                src_ref=pack.at[0, lane], dst_ref=diagonal.at[side, lane],
                send_sem=dia_send.at[side, lane], recv_sem=dia_recv.at[side, lane],
                device_id=(to_gx, g), device_id_type=MESH,
            )
            for lane, g in ((0, west), (1, east))
        ]

    def start_sends(slot):
        for end, pack in ((at_low, pack_lo), (at_high, pack_hi)):

            @pl.when(end)
            def _(pack=pack):
                for g in range(gyn):
                    to_far(pack, slot, g).start()
                for i in range(1, gyn):
                    to_near(pack, slot, i).start()

        @pl.when(not_low)
        def _():
            down(slot).start()

        @pl.when(not_high)
        def _():
            up(slot).start()

    def finish_sends(slot):
        @pl.when(at_end)
        def _():
            for g in range(gyn):
                to_far(pack_lo, slot, g).wait_send()
            for i in range(1, gyn):
                to_near(pack_lo, slot, i).wait_send()

        @pl.when(not_low)
        def _():
            down(slot).wait_send()

        @pl.when(not_high)
        def _():
            up(slot).wait_send()

    to_west = pltpu.make_async_remote_copy(
        src_ref=U.at[:, 0:OWN, :, 0:128], dst_ref=col_r, send_sem=col_send.at[0], recv_sem=col_recv.at[0],
        device_id=(gx, west), device_id_type=MESH,
    )
    to_east = pltpu.make_async_remote_copy(
        src_ref=U.at[:, 0:OWN, :, 128:256], dst_ref=col_l, send_sem=col_send.at[1], recv_sem=col_recv.at[1],
        device_id=(gx, east), device_id_type=MESH,
    )

    for field in range(7):
        for k in range(OWN):
            U[field, k, :, 256:384] = U[field, k, :, 0:128]
        for k in (ABOVE, BELOW) + AHEAD:
            U[field, k] = U[field, 0]
    pack_edges(0)
    pl.semaphore_wait(barrier, jnp.where(at_end, 2 * gyn + 2, 8))

    start_sends(0)

    @pl.when(not_low)
    def _():
        for copy in diagonals(pack_lo, 0, below_gx):
            copy.start()

    @pl.when(not_high)
    def _():
        for copy in diagonals(pack_hi, 1, above_gx):
            copy.start()

    to_west.start()
    to_east.start()

    def first_columns():
        to_west.wait()
        to_east.wait()
        for field in range(7):
            for k in range(OWN):
                U[field, k, :, 256:384] = jnp.where(near, col_r[field, k], col_l[field, k])
        for partner, side, pack, ref, sent_to in ((not_high, 0, pack_lo, recv_hi, not_low), (not_low, 1, pack_hi, recv_lo, not_high)):

            @pl.when(sent_to)
            def _(side=side, pack=pack):
                for copy in diagonals(pack, side, gx):
                    copy.wait_send()

            @pl.when(partner)
            def _(side=side, pack=pack, ref=ref):
                for copy in diagonals(pack, side, gx):
                    copy.wait_recv()
                for part in range(PARTS):
                    ref[0, 2, part] = jnp.where(near, diagonal[side, 0, part], diagonal[side, 1, part])

    def ghosts_of_neighbours(slot):
        @pl.when(not_high)
        def _():
            outer = unpacked(load_pack(recv_hi, slot, (0, 1, 2)), 0)
            inner = unpacked(load_pack(recv_hi, slot, (3, 4, 5)), 3)
            for f in range(7):
                U[f, ABOVE] = jnp.where(rows8 < 3, outer[f], inner[f])

        @pl.when(not_low)
        def _():
            outer = unpacked(load_pack(recv_lo, slot, (0, 1, 2)), 5)
            inner = unpacked(load_pack(recv_lo, slot, (3, 4, 5)), 2)
            for f in range(7):
                U[f, BELOW] = jnp.where(rows8 >= 5, outer[f], inner[f])

    def window(ring, parts, moved):
        origin = lax.rem(gy * 256 + moved + 512 * gyn, 256 * gyn)
        lane_tile = lax.div(origin, 128)
        offset = lax.rem(origin, 128)
        turn = lax.rem(128 - offset, 128)
        inside = lane_iota((8, 128)) < 128 - offset
        out = []
        for part in parts:
            turned = [
                pltpu.roll(ring[lax.rem(lane_tile + (circle - 1 + i), circle), part], turn, 1) for i in range(5)
            ]
            spans = [jnp.where(inside, a, b) for a, b in zip(turned[:-1], turned[1:])]
            out.append(jnp.concatenate([spans[1], spans[2], jnp.where(near, spans[3], spans[0])], axis=1))
        return out

    def blended(x, fraction, towards):
        return (1.0 - fraction) * x + fraction * roll(x, -towards, 1)

    def low_ghosts(f, raw, fraction):
        ghost = blended(raw, fraction, -1)
        far_rows = roll(raw, 1, 0)
        own = roll(blended(U[f, 0], fraction, 1), 1, 0)
        U[f, BELOW] = jnp.where(rows8 >= 5, ghost, jnp.where(first_row, far_rows, own))
        U[f, ABOVE] = jnp.where(rows8 >= 6, far_rows, U[f, ABOVE])

    def high_ghosts(f, raw, fraction):
        ghost = blended(raw, fraction, 1)
        far_rows = roll(raw, 6, 0)
        own = roll(blended(U[f, OWN - 1], fraction, -1), -2, 0)
        U[f, ABOVE] = jnp.where(rows8 < 3, ghost, jnp.where(rows8 < 6, own, far_rows))
        U[f, BELOW] = jnp.where(rows8 < 2, far_rows, U[f, BELOW])

    def ghosts_of_far_end(slot, n):
        @pl.when(at_end)
        def _():
            for i in range(1, gyn):
                from_near(slot, i).wait_recv()
            for g in range(gyn):
                from_far(slot, g).wait_recv()
            for place in range(circle):
                for part in range(PARTS):
                    ring_far[place, part] = circ_far[slot, place, part]

        shift, shift_next = shift_ref[n], shift_ref[n + 1]
        fraction = frac_ref[n]
        A, B = (0, 1, 2), (3, 4, 5)
        left, right = AHEAD

        def near_ring(pack):
            for place in range(circle):
                mine = lax.div(place + 0 * gy, 2) == gy
                for part in range(3):
                    ring_near[place, part] = jnp.where(mine, pack[slot, place % 2, part], circ_near[slot, place, part])

        @pl.when(at_low)
        def _():
            near_ring(pack_lo)
            for f, raw in enumerate(unpacked(window(ring_far, A, -shift), 5)):
                low_ghosts(f, raw, fraction)
            outer = window(ring_far, A, -shift_next)
            inner = unpacked(window(ring_far, B, -shift_next), 2)
            beyond = window(ring_near, A, shift - shift_next)
            rows_a = unpacked(outer, 5)
            ghost = unpacked([blended(x, fraction, 1) for x in beyond], 0)
            mirror = unpacked([blended(x, fraction, -1) for x in outer], 3)
            raw = unpacked(beyond, 6)
            for f in range(7):
                U[f, left] = jnp.where(first_row, raw[f], jnp.where(rows8 < 5, inner[f], rows_a[f]))
                U[f, right] = jnp.where(rows8 < 3, ghost[f], jnp.where(rows8 < 6, mirror[f], raw[f]))

        @pl.when(at_high)
        def _():
            near_ring(pack_hi)
            for f, raw in enumerate(unpacked(window(ring_far, A, shift), 0)):
                high_ghosts(f, raw, fraction)
            outer = window(ring_far, A, shift_next)
            inner = unpacked(window(ring_far, B, shift_next), 3)
            beyond = window(ring_near, A, shift_next - shift)
            rows_a = unpacked(outer, 0)
            ghost = unpacked([blended(x, fraction, -1) for x in beyond], 5)
            mirror = unpacked([blended(x, fraction, 1) for x in outer], 2)
            raw = unpacked(beyond, 7)
            for f in range(7):
                U[f, left] = jnp.where(rows8 < 2, raw[f], jnp.where(rows8 < 5, mirror[f], ghost[f]))
                U[f, right] = jnp.where(rows8 < 3, rows_a[f], jnp.where(last_row, raw[f], inner[f]))

    def ghosts_from_ahead(n):
        fraction = frac_ref[n]

        @pl.when(at_low)
        def _():
            for f in range(7):
                low_ghosts(f, U[f, AHEAD[0]], fraction)

        @pl.when(at_high)
        def _():
            for f in range(7):
                high_ghosts(f, U[f, AHEAD[1]], fraction)

    def minmod(a, b):
        return jnp.maximum(jnp.minimum(a, b), 0.0) + jnp.minimum(jnp.maximum(a, b), 0.0)

    def signal(density, speed, squared):
        total = density + squared
        return jnp.abs(speed) + jnp.abs(total) * lax.rsqrt(total * density)

    def riemann(left, right, normal, wanted):
        dl, vnl, vtl, vsl, btl, bsl = left
        dr, vnr, vtr, vsr, btr, bsr = right
        n2 = normal * normal
        tl = btl * btl + bsl * bsl
        tr = btr * btr + bsr * bsr
        fastest = jnp.maximum(signal(dl, vnl, n2 + tl), signal(dr, vnr, n2 + tr))
        ul = vnl + fastest
        ur = vnr - fastest
        out = {}
        if wanted != (4,):
            al = dl * ul
            ar = dr * ur
        if 0 in wanted:
            out[0] = al + ar
        if 1 in wanted:
            out[1] = (al * vnl + ar * vnr) + ((dl + dr) + (0.5 * (tl + tr) - n2))
        if 2 in wanted:
            out[2] = (al * vtl + ar * vtr) - normal * (btl + btr)
        if 3 in wanted:
            out[3] = (al * vsl + ar * vsr) - normal * (bsl + bsr)
        if 4 in wanted:
            out[4] = (btl * ul + btr * ur) - normal * (vtl + vtr)
        if 5 in wanted:
            out[5] = (bsl * ul + bsr * ur) - normal * (vsl + vsr)
        return out

    def primitives(k, density, mx, my, mz, bz, bx, bx_after, by):
        inverse = 1.0 / density
        Q[0, k] = density
        Q[VX, k] = mx * inverse
        Q[VY, k] = my * inverse
        Q[VZ, k] = mz * inverse
        Q[CX, k] = 0.5 * (bx + row_after(bx, bx_after))
        Q[CY, k] = 0.5 * (by + lane_after(by))
        Q[QBZ, k] = bz

    def initial_primitives(k):
        primitives(k, *(U[f, k] for f in (D, MX, MY, MZ, BZ, BX)), U[BX, following(k)], U[BY, k])

    X_STATE = (0, VX, VY, VZ, CY, QBZ)
    Y_STATE = (0, VY, VX, VZ, CX, QBZ)

    def finish_fluxes(k, fx, fy, stride, mx, my, cells):
        half = 0.5 * stride
        if 0 in fx:
            for spot, part in enumerate((0, 1, 2, 3, 5)):
                FX[spot, k] = fx[part]
        FY4[k] = fy[4]
        SX4[k] = fx[4] + lane_before(fx[4])
        if cells:
            for spot, (field, px, py) in enumerate(((D, 0, 0), (MX, 1, 2), (MY, 2, 1), (MZ, 3, 3), (BZ, 5, 5))):
                value = U[field, k] - half * ((lane_after(fy[py]) - fy[py]) - fx[px])
                if field == MX:
                    value += (stride * 2.0 * OMEGA) * my
                if field == MY:
                    value -= (stride * (2.0 - QSHEAR) * OMEGA) * mx
                PART[spot, k] = value

    ALL = (0, 1, 2, 3, 4, 5)

    def first_order(k, stride):
        left = [row_before(Q[i, previous(k)], Q[i, k]) for i in X_STATE]
        fx = riemann(left, [Q[i, k] for i in X_STATE], U[BX, k], ALL)
        right = [Q[i, k] for i in Y_STATE]
        fy = riemann([lane_before(q) for q in right], right, U[BY, k], ALL)
        finish_fluxes(k, fx, fy, stride, U[MX, k], U[MY, k], True)

    def slopes(k):
        for spot, i in enumerate(X_STATE):
            here = Q[i, k]
            gradient = 0.5 * minmod(here - row_before(Q[i, previous(k)], here), row_after(here, Q[i, following(k)]) - here)
            QL[spot, k] = here + gradient
            QR[spot, k] = here - gradient

    def second_order(k, stride, last):
        cells = k < OWN or not last
        x_wanted = ALL if cells or k == ABOVE else (4,)
        y_wanted = ALL if cells else (4,)
        left = [row_before(QL[i, previous(k)], QL[i, k]) for i in range(6)]
        fx = riemann(left, [QR[i, k] for i in range(6)], NBX[k], x_wanted)
        left, right = [], []
        for i in Y_STATE:
            here = Q[i, k]
            behind = here - lane_before(here)
            gradient = 0.5 * minmod(behind, lane_after(behind))
            left.append(lane_before(here + gradient))
            right.append(here - gradient)
        fy = riemann(left, right, NBY[k], y_wanted)
        finish_fluxes(k, fx, fy, stride, M[0, k], M[1, k], cells)

    def corner(k):
        return 0.125 * (FY4[k] + row_before(FY4[previous(k)], FY4[k]) - SX4[k])

    def face_x(k, emf, stride):
        EZ[k] = emf
        return U[BX, k] - stride * (lane_after(emf) - emf)

    def face_y(k, stride):
        emf = EZ[k]
        return U[BY, k] + stride * (row_after(emf, EZ[following(k)]) - emf)

    def cells_of(k, stride):
        return [PART[i, k] - (0.5 * stride) * row_after(FX[i, k], FX[i, following(k)]) for i in range(5)]

    def advance(n, last):
        fraction = frac_ref[n]

        def tiles(run):
            for k in range(RING):
                run(k)
            if not last:

                @pl.when(at_end)
                def _():
                    for k in AHEAD:
                        run(k)

        stride = 0.5 * TIMESTEP
        tiles(initial_primitives)
        tiles(lambda k: first_order(k, stride))

        def predicted_x(k):
            NBX[k] = face_x(k, corner(k), stride)

        tiles(predicted_x)

        def predicted_cells(k):
            density, mx, my, mz, bz = cells_of(k, stride)
            by = face_y(k, stride)
            NBY[k] = by
            M[0, k] = mx
            M[1, k] = my
            primitives(k, density, mx, my, mz, bz, NBX[k], NBX[following(k)], by)

        tiles(predicted_cells)

        tiles(slopes)
        tiles(lambda k: second_order(k, TIMESTEP, last))
        kept = range(OWN) if last else range(RING)

        def mended(emf, remote_row, towards, ours):
            remote = blended(remote_row, fraction, towards)
            return jnp.where(jnp.logical_and(first_row, ours), 0.5 * (emf + remote), emf)

        emfs = [corner(k) for k in range(RING)]
        low_fix = mended(emfs[0], roll(emfs[BELOW], -1, 0), -1, at_low)
        high_fix = mended(emfs[ABOVE], roll(emfs[ABOVE], -6, 0), 1, at_high)
        emfs[0], emfs[ABOVE] = low_fix, high_fix
        for k in range(RING):
            new_bx = face_x(k, emfs[k], TIMESTEP)
            if k in kept:
                U[BX, k] = new_bx

        def new_cells(k):
            for field, value in zip((D, MX, MY, MZ, BZ), cells_of(k, TIMESTEP)):
                U[field, k] = value
            U[BY, k] = face_y(k, TIMESTEP)

        for k in kept:
            new_cells(k)
        if not last:

            @pl.when(at_end)
            def _():
                left, right = AHEAD
                emf_l, emf_r = corner(left), corner(right)
                from_low = blended(roll(emf_r, -6, 0), fraction, 1)
                from_high = blended(roll(emf_l, -2, 0), fraction, -1)
                remote = jnp.where(at_low, from_low, from_high)
                emf_r = jnp.where(first_row, 0.5 * (emf_r + remote), emf_r)
                U[BX, left] = face_x(left, emf_l, TIMESTEP)
                U[BX, right] = face_x(right, emf_r, TIMESTEP)
                for k in AHEAD:
                    new_cells(k)

    rounds = STEPS // 2

    def two_steps(r, carry):
        slot = lax.rem(r, 2)

        @pl.when(not_high)
        def _():
            down(slot).wait_recv()

        @pl.when(not_low)
        def _():
            up(slot).wait_recv()

        @pl.when(r == 0)
        def _():
            first_columns()

        ghosts_of_neighbours(slot)
        ghosts_of_far_end(slot, 2 * r)
        advance(2 * r, False)
        ghosts_from_ahead(2 * r + 1)
        advance(2 * r + 1, True)
        finish_sends(slot)

        @pl.when(r < rounds - 1)
        def _():
            pack_edges(1 - slot)
            start_sends(1 - slot)

        return carry

    lax.fori_loop(0, rounds, two_steps, 0)

    for k in range(OWN):
        rows = pl.ds(8 * k, 8)
        den_out[rows, :] = U[D, k, :, 0:256]
        for i, field in enumerate((MX, MY, MZ)):
            mom_out[i, rows, :] = U[field, k, :, 0:256]
        for i, field in enumerate((BX, BY, BZ)):
            mag_out[i, rows, :] = U[field, k, :, 0:256]


def scratch(gyn):
    tile = (TILES, 8, LANES)
    f32 = jnp.float32
    vmem = lambda *shape: pltpu.VMEM(shape, f32)
    dma = pltpu.SemaphoreType.DMA
    return [
        vmem(7, *tile), vmem(7, *tile), vmem(2, *tile), vmem(6, *tile), vmem(6, *tile), vmem(5, *tile), vmem(5, *tile),
        vmem(*tile), vmem(*tile), vmem(*tile), vmem(*tile), vmem(*tile),
        *(vmem(2, 3, PARTS, 8, 128) for _ in range(4)), vmem(2, 2, PARTS, 8, 128),
        vmem(2, 2 * gyn, PARTS, 8, 128), vmem(2, 2 * gyn, 3, 8, 128),
        vmem(2 * gyn, PARTS, 8, 128), vmem(2 * gyn, 3, 8, 128), vmem(7, OWN, 8, 128), vmem(7, OWN, 8, 128),
        pltpu.SMEM((STEPS,), jnp.int32), pltpu.SMEM((STEPS,), f32), dma((5,)),
        dma((2,)), dma((2,)), dma((2,)), dma((2, 2)), dma((2, 2)), dma((2, 2)),
        dma((gyn,)), dma((2, gyn)), dma((gyn,)), dma((2, gyn)),
    ]


def solution(mesh):
    gxn, gyn = mesh.shape["gx"], mesh.shape["gy"]

    def per_device(density, momentum, magnetic, shear_shift, shear_frac):
        return pl.pallas_call(
            functools.partial(kernel, gxn, gyn),
            name="shearing_box",
            out_shape=tuple(jax.ShapeDtypeStruct(a.shape, jnp.float32) for a in (density, momentum, magnetic)),
            in_specs=[pl.BlockSpec(memory_space=pl.ANY)] * 5,
            out_specs=tuple(pl.BlockSpec(memory_space=pltpu.VMEM) for _ in range(3)),
            scratch_shapes=scratch(gyn),
            compiler_params=pltpu.CompilerParams(
                collective_id=0, has_side_effects=True, vmem_limit_bytes=48 * 1024 * 1024
            ),
        )(
            shear_shift,
            shear_frac,
            density.reshape(OWN, 8, 256),
            momentum.reshape(3, OWN, 8, 256),
            magnetic.reshape(3, OWN, 8, 256),
        )

    return jax.shard_map(
        per_device,
        mesh=mesh,
        in_specs=(P("gx", "gy"), P(None, "gx", "gy"), P(None, "gx", "gy"), P(), P()),
        out_specs=(P("gx", "gy"), P(None, "gx", "gy"), P(None, "gx", "gy")),
        check_vma=False,
    )
```

time: 95.6 us -> 82.5 us (0.86)
  Pallas kernels: 88.9 us -> 76.5 us
    pallas_call x1, Pallas kernels: 88.9 us -> 76.5 us  [per_device(): pl.pallas_call(functools.partial(kernel, gxn, gyn), name='shearing_box',...]
where the time goes in v1:
time: 82.5 us; the launch traced here: 82.3 us
  Pallas kernels  76.5 us (93%)
  local copies, waits for them, and re-layouts  5.09 us (6%)
    pallas_call x1, Pallas kernels, per_device(): pl.pallas_call(functools.partial(kernel, gxn, gyn), name='shearing_box',...  76.5 us
    unnamed x13, local copies, waits for them, and re-layouts  5.09 us

profile of v1, /device:TPU:0, one launch (start us, length us, event | category | flops | bytes accessed | tf_op | source)
XLA Modules:
  0.0 82.3 jit_solution(5311869078508459328)
XLA Ops:
  0.6 0.0 copy-start.3
  0.6 0.0 copy-start.4
  0.7 0.6 copy-done.3
  1.3 0.0 copy-done.4
  1.3 0.0 copy-start
  1.3 0.9 %copy-done = f32[3,32,256]{2,1,0:T(8,128)S(1)} copy-done((f32[3,32,256]{2,1,0:T(8,128)S(1)}, f32[3,32,256]{2,1,0:T(8,128)}, u32[]{:S(2)}) %copy-start) | copy-done | bytes 98328
  2.2 0.0 copy-start.1
  2.2 0.9 %copy-done.1 = f32[3,32,256]{2,1,0:T(8,128)S(1)} copy-done((f32[3,32,256]{2,1,0:T(8,128)S(1)}, f32[3,32,256]{2,1,0:T(8,128)}, u32[]{:S(2)}) %copy-start.1) | copy-done | bytes 98328
  3.1 0.0 copy-start.2
  3.1 0.8 copy-done.2
  3.8 76.5 %shearing_box.1 = (f32[32,256]{1,0:T(8,128)S(1)}, f32[3,32,256]{2,1,0:T(8,128)S(1)}, f32[3,32,256]{2,1,0:T(8,128)S(1)}) custom-call(s32[8]{0:T(128)S(1)} %copy-done.3, f32[8]{0:T(128)S(1)} %copy-done.4, f32[4,8,256]{2,1,0:T(8,128)S(1)} %bitcast.5, f32[3,4,8,256]{3,2,1,0:T(8,128)S(1)} %bitcast.3, f32[3,4,8,256]{3,2,1,0:T(8,128)S(1)} %bitcast.4), custom_call_target="tpu_custom_call" | custom-call | tf_op jit(solution)/shard_map/shearing_box/pallas_call | solution.py:653
  80.4 0.6 copy.11
  81.0 0.6 copy.12
  81.6 0.6 copy.13
Async XLA Ops:
  0.6 0.7 copy-start.3
  0.6 0.7 copy-start.4
  1.3 0.9 %copy-start = (f32[3,32,256]{2,1,0:T(8,128)S(1)}, f32[3,32,256]{2,1,0:T(8,128)}, u32[]{:S(2)}) copy-start(f32[3,32,256]{2,1,0:T(8,128)} %param.6) | copy-start | bytes 294916
  2.2 0.9 %copy-start.1 = (f32[3,32,256]{2,1,0:T(8,128)S(1)}, f32[3,32,256]{2,1,0:T(8,128)}, u32[]{:S(2)}) copy-start(f32[3,32,256]{2,1,0:T(8,128)} %param.7) | copy-start | bytes 294916
  3.1 0.8 copy-start.2

commit v2 on v1

--- a/solution.py
+++ b/solution.py
@@ -39,9 +39,9 @@
 def kernel(
     gxn, gyn, shift_in, frac_in, den, mom, mag, den_out, mom_out, mag_out,
     U, Q, M, QL, QR, FX, PART, FY4, SX4, EZ, NBX, NBY,
-    pack_lo, pack_hi, recv_lo, recv_hi, diagonal, circ_far, circ_near, ring_far, ring_near, col_r, col_l,
+    pack_lo, pack_hi, recv_lo, recv_hi, block, circ_far, circ_near, ring_far, ring_near, col_r, col_l,
     shift_ref, frac_ref, load_sem,
-    col_send, col_recv, row_send, row_recv, dia_send, dia_recv, far_send, far_recv, near_send, near_recv,
+    col_send, col_recv, row_send, row_recv, far_send, far_recv, near_send, near_recv,
 ):
     gx = lax.axis_index("gx")
     gy = lax.axis_index("gy")
@@ -55,7 +55,6 @@
     other_end = gxn - 1 - gx
     east = lax.rem(gy + 1, gyn)
     west = lax.rem(gy + gyn - 1, gyn)
-    circle = 2 * gyn
 
     rows8 = row_iota((8, LANES))
     first_row = rows8 == 0
@@ -75,15 +74,20 @@
         return roll(jnp.where(first_row, after, here), -1, 0)
 
     def lane_before(x):
-        return roll(x, 1, 1)
+        return jnp.concatenate([roll(x[:, 256:384], 1, 1), x[:, 0:128], x[:, 128:256]], axis=1)
 
     def lane_after(x):
-        return roll(x, -1, 1)
+        return jnp.concatenate([x[:, 128:256], x[:, 256:384], roll(x[:, 0:128], -1, 1)], axis=1)
+
+    spots = lane_iota((8, LANES))
+    columns = 3 * (spots & 127) + (spots >> 7)
+    spot_of_row = lane_iota((LANES, LANES))
+    permutation = jnp.where(row_iota((LANES, LANES)) == 3 * (spot_of_row & 127) + (spot_of_row >> 7), 1.0, 0.0)
 
     loads = [
-        pltpu.make_async_copy(den, U.at[D, 0:OWN, :, 0:256], load_sem.at[0]),
-        pltpu.make_async_copy(mom, U.at[MX : MZ + 1, 0:OWN, :, 0:256], load_sem.at[1]),
-        pltpu.make_async_copy(mag, U.at[BX : BZ + 1, 0:OWN, :, 0:256], load_sem.at[2]),
+        pltpu.make_async_copy(den, block.at[D], load_sem.at[0]),
+        pltpu.make_async_copy(mom, block.at[MX : MZ + 1], load_sem.at[1]),
+        pltpu.make_async_copy(mag, block.at[BX : BZ + 1], load_sem.at[2]),
         pltpu.make_async_copy(shift_in, shift_ref, load_sem.at[3]),
         pltpu.make_async_copy(frac_in, frac_ref, load_sem.at[4]),
     ]
@@ -109,13 +113,11 @@
 
     @pl.when(not_low)
     def _():
-        for g in (west, gy, east):
-            greet(below_gx, g)
+        greet(below_gx, gy)
 
     @pl.when(not_high)
     def _():
-        for g in (west, gy, east):
-            greet(above_gx, g)
+        greet(above_gx, gy)
 
     for load in loads:
         load.wait()
@@ -153,23 +155,23 @@
         pack_edge(pack_lo, slot, 0, 0, 3)
         pack_edge(pack_hi, slot, OWN - 1, 5, 2)
 
-    def to_far(pack, slot, g):
+    def to_far(pack, source, slot, g):
         return pltpu.make_async_remote_copy(
-            src_ref=pack.at[slot, 0:2], dst_ref=circ_far.at[slot, pl.ds(2 * gy, 2)],
+            src_ref=pack.at[source], dst_ref=circ_far.at[slot, gy],
             send_sem=far_send.at[g], recv_sem=far_recv.at[slot, gy],
             device_id=(other_end, g), device_id_type=MESH,
         )
 
     def from_far(slot, g):
         return pltpu.make_async_remote_copy(
-            src_ref=pack_lo.at[slot, 0:2], dst_ref=circ_far.at[slot, pl.ds(2 * g, 2)],
+            src_ref=pack_lo.at[slot], dst_ref=circ_far.at[slot, g],
             send_sem=far_send.at[g], recv_sem=far_recv.at[slot, g],
             device_id=(other_end, g), device_id_type=MESH,
         )
 
-    def to_near(pack, slot, i):
+    def to_near(pack, source, slot, i):
         return pltpu.make_async_remote_copy(
-            src_ref=pack.at[slot, 0:2, 0:3], dst_ref=circ_near.at[slot, pl.ds(2 * gy, 2)],
+            src_ref=pack.at[source, :, 0:3], dst_ref=circ_near.at[slot, gy],
             send_sem=near_send.at[i], recv_sem=near_recv.at[slot, i],
             device_id=(gx, lax.rem(gy + i, gyn)), device_id_type=MESH,
         )
@@ -177,7 +179,7 @@
     def from_near(slot, i):
         sender = lax.rem(gy + gyn - i, gyn)
         return pltpu.make_async_remote_copy(
-            src_ref=pack_lo.at[slot, 0:2, 0:3], dst_ref=circ_near.at[slot, pl.ds(2 * sender, 2)],
+            src_ref=pack_lo.at[slot, :, 0:3], dst_ref=circ_near.at[slot, sender],
             send_sem=near_send.at[i], recv_sem=near_recv.at[slot, i],
             device_id=(gx, sender), device_id_type=MESH,
         )
@@ -194,26 +196,17 @@
             device_id=(above_gx, gy), device_id_type=MESH,
         )
 
-    def diagonals(pack, side, to_gx):
-        return [
-            pltpu.make_async_remote_copy(
-                src_ref=pack.at[0, lane], dst_ref=diagonal.at[side, lane],
-                send_sem=dia_send.at[side, lane], recv_sem=dia_recv.at[side, lane],
-                device_id=(to_gx, g), device_id_type=MESH,
-            )
-            for lane, g in ((0, west), (1, east))
-        ]
-
-    def start_sends(slot):
+    def start_far(source, slot):
         for end, pack in ((at_low, pack_lo), (at_high, pack_hi)):
 
             @pl.when(end)
             def _(pack=pack):
                 for g in range(gyn):
-                    to_far(pack, slot, g).start()
+                    to_far(pack, source, slot, g).start()
                 for i in range(1, gyn):
-                    to_near(pack, slot, i).start()
-
+                    to_near(pack, source, slot, i).start()
+
+    def start_rows(slot):
         @pl.when(not_low)
         def _():
             down(slot).start()
@@ -226,9 +219,9 @@
         @pl.when(at_end)
         def _():
             for g in range(gyn):
-                to_far(pack_lo, slot, g).wait_send()
+                to_far(pack_lo, slot, slot, g).wait_send()
             for i in range(1, gyn):
-                to_near(pack_lo, slot, i).wait_send()
+                to_near(pack_lo, slot, slot, i).wait_send()
 
         @pl.when(not_low)
         def _():
@@ -239,56 +232,40 @@
             up(slot).wait_send()
 
     to_west = pltpu.make_async_remote_copy(
-        src_ref=U.at[:, 0:OWN, :, 0:128], dst_ref=col_r, send_sem=col_send.at[0], recv_sem=col_recv.at[0],
+        src_ref=block.at[:, :, :, 0:128], dst_ref=col_r, send_sem=col_send.at[0], recv_sem=col_recv.at[0],
         device_id=(gx, west), device_id_type=MESH,
     )
     to_east = pltpu.make_async_remote_copy(
-        src_ref=U.at[:, 0:OWN, :, 128:256], dst_ref=col_l, send_sem=col_send.at[1], recv_sem=col_recv.at[1],
+        src_ref=block.at[:, :, :, 128:256], dst_ref=col_l, send_sem=col_send.at[1], recv_sem=col_recv.at[1],
         device_id=(gx, east), device_id_type=MESH,
     )
 
+    def interleaved(x, start, stop):
+        flat = x.reshape(7 * OWN * 8, stop - start)
+        out = jnp.dot(
+            flat, permutation[start:stop], precision=lax.Precision.HIGHEST, preferred_element_type=jnp.float32
+        )
+        return out.reshape(7, OWN, 8, LANES)
+
+    own_columns = interleaved(block[...], 0, 256)
+    U[:, 0:OWN] = own_columns
+    pack_edges(1)
+    pl.semaphore_wait(barrier, jnp.where(at_end, 2 * gyn, 4))
+
+    start_far(1, 0)
+    to_west.start()
+    to_east.start()
+    to_west.wait()
+    to_east.wait()
+
+    near = lane_iota((7, OWN, 8, 128)) < 64
+    halo = interleaved(jnp.where(near, col_r[...], col_l[...]), 256, 384)
+    U[:, 0:OWN] = U[:, 0:OWN] + halo
     for field in range(7):
-        for k in range(OWN):
-            U[field, k, :, 256:384] = U[field, k, :, 0:128]
         for k in (ABOVE, BELOW) + AHEAD:
             U[field, k] = U[field, 0]
     pack_edges(0)
-    pl.semaphore_wait(barrier, jnp.where(at_end, 2 * gyn + 2, 8))
-
-    start_sends(0)
-
-    @pl.when(not_low)
-    def _():
-        for copy in diagonals(pack_lo, 0, below_gx):
-            copy.start()
-
-    @pl.when(not_high)
-    def _():
-        for copy in diagonals(pack_hi, 1, above_gx):
-            copy.start()
-
-    to_west.start()
-    to_east.start()
-
-    def first_columns():
-        to_west.wait()
-        to_east.wait()
-        for field in range(7):
-            for k in range(OWN):
-                U[field, k, :, 256:384] = jnp.where(near, col_r[field, k], col_l[field, k])
-        for partner, side, pack, ref, sent_to in ((not_high, 0, pack_lo, recv_hi, not_low), (not_low, 1, pack_hi, recv_lo, not_high)):
-
-            @pl.when(sent_to)
-            def _(side=side, pack=pack):
-                for copy in diagonals(pack, side, gx):
-                    copy.wait_send()
-
-            @pl.when(partner)
-            def _(side=side, pack=pack, ref=ref):
-                for copy in diagonals(pack, side, gx):
-                    copy.wait_recv()
-                for part in range(PARTS):
-                    ref[0, 2, part] = jnp.where(near, diagonal[side, 0, part], diagonal[side, 1, part])
+    start_rows(0)
 
     def ghosts_of_neighbours(slot):
         @pl.when(not_high)
@@ -305,23 +282,36 @@
             for f in range(7):
                 U[f, BELOW] = jnp.where(rows8 >= 5, outer[f], inner[f])
 
+    wrapped = jnp.where(columns < 320, columns, columns - LANES)
+
     def window(ring, parts, moved):
         origin = lax.rem(gy * 256 + moved + 512 * gyn, 256 * gyn)
-        lane_tile = lax.div(origin, 128)
-        offset = lax.rem(origin, 128)
-        turn = lax.rem(128 - offset, 128)
-        inside = lane_iota((8, 128)) < 128 - offset
+        first_block = lax.div(origin, 256)
+        offset = lax.rem(origin, 256)
+        sources = []
+        for i in (0, 1, jnp.where(offset < 128, -1, 2)):
+            ahead = offset - 256 * i
+            whole = lax.div(ahead + 2 * LANES, 3)
+            phase = lax.rem(ahead + 2 * LANES, 3)
+            place = lax.rem(first_block + i + gyn, gyn)
+            picks = []
+            for j in range(3):
+                vector = lax.rem(phase + j, 3)
+                turn = lax.rem(4 * 128 - whole - lax.div(phase + j, 3), 128)
+                picks.append((vector, turn))
+            at = wrapped + ahead
+            sources.append((place, picks, jnp.logical_and(at >= 0, at < 256)))
         out = []
         for part in parts:
-            turned = [
-                pltpu.roll(ring[lax.rem(lane_tile + (circle - 1 + i), circle), part], turn, 1) for i in range(5)
+            spans = [
+                jnp.concatenate([pltpu.roll(ring[place, vector, part], turn, 1) for vector, turn in picks], axis=1)
+                for place, picks, _ in sources
             ]
-            spans = [jnp.where(inside, a, b) for a, b in zip(turned[:-1], turned[1:])]
-            out.append(jnp.concatenate([spans[1], spans[2], jnp.where(near, spans[3], spans[0])], axis=1))
+            out.append(jnp.where(sources[0][2], spans[0], jnp.where(sources[1][2], spans[1], spans[2])))
         return out
 
     def blended(x, fraction, towards):
-        return (1.0 - fraction) * x + fraction * roll(x, -towards, 1)
+        return (1.0 - fraction) * x + fraction * (lane_after(x) if towards == 1 else lane_before(x))
 
     def low_ghosts(f, raw, fraction):
         ghost = blended(raw, fraction, -1)
@@ -344,24 +334,18 @@
                 from_near(slot, i).wait_recv()
             for g in range(gyn):
                 from_far(slot, g).wait_recv()
-            for place in range(circle):
-                for part in range(PARTS):
-                    ring_far[place, part] = circ_far[slot, place, part]
+            for place in range(gyn):
+                ring_far[place] = circ_far[slot, place]
+                ring_near[place] = circ_near[slot, place]
 
         shift, shift_next = shift_ref[n], shift_ref[n + 1]
         fraction = frac_ref[n]
         A, B = (0, 1, 2), (3, 4, 5)
         left, right = AHEAD
 
-        def near_ring(pack):
-            for place in range(circle):
-                mine = lax.div(place + 0 * gy, 2) == gy
-                for part in range(3):
-                    ring_near[place, part] = jnp.where(mine, pack[slot, place % 2, part], circ_near[slot, place, part])
-
         @pl.when(at_low)
         def _():
-            near_ring(pack_lo)
+            ring_near[gy] = pack_lo[slot, :, 0:3]
             for f, raw in enumerate(unpacked(window(ring_far, A, -shift), 5)):
                 low_ghosts(f, raw, fraction)
             outer = window(ring_far, A, -shift_next)
@@ -377,7 +361,7 @@
 
         @pl.when(at_high)
         def _():
-            near_ring(pack_hi)
+            ring_near[gy] = pack_hi[slot, :, 0:3]
             for f, raw in enumerate(unpacked(window(ring_far, A, shift), 0)):
                 high_ghosts(f, raw, fraction)
             outer = window(ring_far, A, shift_next)
@@ -600,10 +584,6 @@
         def _():
             up(slot).wait_recv()
 
-        @pl.when(r == 0)
-        def _():
-            first_columns()
-
         ghosts_of_neighbours(slot)
         ghosts_of_far_end(slot, 2 * r)
         advance(2 * r, False)
@@ -614,19 +594,21 @@
         @pl.when(r < rounds - 1)
         def _():
             pack_edges(1 - slot)
-            start_sends(1 - slot)
+            start_far(1 - slot, 1 - slot)
+            start_rows(1 - slot)
 
         return carry
 
     lax.fori_loop(0, rounds, two_steps, 0)
 
-    for k in range(OWN):
-        rows = pl.ds(8 * k, 8)
-        den_out[rows, :] = U[D, k, :, 0:256]
-        for i, field in enumerate((MX, MY, MZ)):
-            mom_out[i, rows, :] = U[field, k, :, 0:256]
-        for i, field in enumerate((BX, BY, BZ)):
-            mag_out[i, rows, :] = U[field, k, :, 0:256]
+    flat = U[:, 0:OWN].reshape(7 * OWN * 8, LANES)
+    out = lax.dot_general(
+        flat, permutation[0:256], (((1,), (1,)), ((), ())),
+        precision=lax.Precision.HIGHEST, preferred_element_type=jnp.float32,
+    ).reshape(7, 8 * OWN, 256)
+    den_out[...] = out[D]
+    mom_out[...] = out[MX : MZ + 1]
+    mag_out[...] = out[BX : BZ + 1]
 
 
 def scratch(gyn):
@@ -637,11 +619,11 @@
     return [
         vmem(7, *tile), vmem(7, *tile), vmem(2, *tile), vmem(6, *tile), vmem(6, *tile), vmem(5, *tile), vmem(5, *tile),
         vmem(*tile), vmem(*tile), vmem(*tile), vmem(*tile), vmem(*tile),
-        *(vmem(2, 3, PARTS, 8, 128) for _ in range(4)), vmem(2, 2, PARTS, 8, 128),
-        vmem(2, 2 * gyn, PARTS, 8, 128), vmem(2, 2 * gyn, 3, 8, 128),
-        vmem(2 * gyn, PARTS, 8, 128), vmem(2 * gyn, 3, 8, 128), vmem(7, OWN, 8, 128), vmem(7, OWN, 8, 128),
+        *(vmem(2, 3, PARTS, 8, 128) for _ in range(4)), vmem(7, OWN, 8, 256),
+        vmem(2, gyn, 3, PARTS, 8, 128), vmem(2, gyn, 3, 3, 8, 128),
+        vmem(gyn, 3, PARTS, 8, 128), vmem(gyn, 3, 3, 8, 128), vmem(7, OWN, 8, 128), vmem(7, OWN, 8, 128),
         pltpu.SMEM((STEPS,), jnp.int32), pltpu.SMEM((STEPS,), f32), dma((5,)),
-        dma((2,)), dma((2,)), dma((2,)), dma((2, 2)), dma((2, 2)), dma((2, 2)),
+        dma((2,)), dma((2,)), dma((2,)), dma((2, 2)),
         dma((gyn,)), dma((2, gyn)), dma((gyn,)), dma((2, gyn)),
     ]
 

time: 82.5 us -> 75.9 us (0.920)
  Pallas kernels: 76.5 us -> 69.9 us
    pallas_call x1, Pallas kernels: 76.5 us -> 69.9 us  [per_device(): pl.pallas_call(functools.partial(kernel, gxn, gyn), name='shearing_box',...]
where the time goes in v2:
time: 75.9 us; the launch traced here: 75.6 us
  Pallas kernels  69.9 us (92%)
  local copies, waits for them, and re-layouts  5.09 us (7%)
    pallas_call x1, Pallas kernels, per_device(): pl.pallas_call(functools.partial(kernel, gxn, gyn), name='shearing_box',...  69.9 us
    unnamed x13, local copies, waits for them, and re-layouts  5.09 us

profile of v2, /device:TPU:0, one launch (start us, length us, event | category | flops | bytes accessed | tf_op | source)
XLA Modules:
  0.0 75.6 jit_solution(14717088623942624877)
XLA Ops:
  0.6 0.0 copy-start.3
  0.6 0.0 copy-start.4
  0.7 0.6 copy-done.3
  1.3 0.0 copy-done.4
  1.3 0.0 copy-start
  1.3 0.9 %copy-done = f32[3,32,256]{2,1,0:T(8,128)S(1)} copy-done((f32[3,32,256]{2,1,0:T(8,128)S(1)}, f32[3,32,256]{2,1,0:T(8,128)}, u32[]{:S(2)}) %copy-start) | copy-done | bytes 98328
  2.2 0.0 copy-start.1
  2.2 0.9 %copy-done.1 = f32[3,32,256]{2,1,0:T(8,128)S(1)} copy-done((f32[3,32,256]{2,1,0:T(8,128)S(1)}, f32[3,32,256]{2,1,0:T(8,128)}, u32[]{:S(2)}) %copy-start.1) | copy-done | bytes 98328
  3.1 0.0 copy-start.2
  3.1 0.8 copy-done.2
  3.8 69.9 %shearing_box.1 = (f32[32,256]{1,0:T(8,128)S(1)}, f32[3,32,256]{2,1,0:T(8,128)S(1)}, f32[3,32,256]{2,1,0:T(8,128)S(1)}) custom-call(s32[8]{0:T(128)S(1)} %copy-done.3, f32[8]{0:T(128)S(1)} %copy-done.4, f32[4,8,256]{2,1,0:T(8,128)S(1)} %bitcast.5, f32[3,4,8,256]{3,2,1,0:T(8,128)S(1)} %bitcast.3, f32[3,4,8,256]{3,2,1,0:T(8,128)S(1)} %bitcast.4), custom_call_target="tpu_custom_call" | custom-call | tf_op jit(solution)/shard_map/shearing_box/pallas_call | solution.py:635
  73.7 0.6 copy.11
  74.4 0.6 copy.12
  75.0 0.6 copy.13
Async XLA Ops:
  0.6 0.7 copy-start.3
  0.6 0.7 copy-start.4
  1.3 0.9 %copy-start = (f32[3,32,256]{2,1,0:T(8,128)S(1)}, f32[3,32,256]{2,1,0:T(8,128)}, u32[]{:S(2)}) copy-start(f32[3,32,256]{2,1,0:T(8,128)} %param.6) | copy-start | bytes 294916
  2.2 0.9 %copy-start.1 = (f32[3,32,256]{2,1,0:T(8,128)S(1)}, f32[3,32,256]{2,1,0:T(8,128)}, u32[]{:S(2)}) copy-start(f32[3,32,256]{2,1,0:T(8,128)} %param.7) | copy-start | bytes 294916
  3.1 0.8 %copy-start.2 = (f32[32,256]{1,0:T(8,128)S(1)}, f32[32,256]{1,0:T(8,128)}, u32[]{:S(2)}) copy-start(f32[32,256]{1,0:T(8,128)} %param.5) | copy-start | bytes 98308

commit v3 on v2

--- a/solution.py
+++ b/solution.py
@@ -19,9 +19,10 @@
 ABOVE, BELOW = OWN, OWN + 1
 RING = OWN + 2
 AHEAD = (RING, RING + 1)
+MAIN = tuple(range(RING))
 TILES = RING + 2
 LANES = 384
-PARTS = 6
+GROUPS = 2
 
 
 def roll(x, shift, axis):
@@ -144,34 +145,35 @@
 
     def pack_edge(ref, slot, k, outer, inner):
         tiles = [U[f, k] for f in range(7)]
-        for part, tile in enumerate(packed(tiles, outer) + packed(tiles, inner)):
-            for lane in range(3):
-                ref[slot, lane, part] = tile[:, 128 * lane : 128 * (lane + 1)]
-
-    def load_pack(ref, slot, parts):
-        return [jnp.concatenate([ref[slot, lane, part] for lane in range(3)], axis=1) for part in parts]
+        for group, first in enumerate((outer, inner)):
+            for part, tile in enumerate(packed(tiles, first)):
+                for lane in range(3):
+                    ref[slot, group, lane, part] = tile[:, 128 * lane : 128 * (lane + 1)]
+
+    def load_pack(ref, slot, group):
+        return [jnp.concatenate([ref[slot, group, lane, part] for lane in range(3)], axis=1) for part in range(3)]
 
     def pack_edges(slot):
         pack_edge(pack_lo, slot, 0, 0, 3)
         pack_edge(pack_hi, slot, OWN - 1, 5, 2)
 
-    def to_far(pack, source, slot, g):
+    def to_far(pack, source, slot, group, g):
         return pltpu.make_async_remote_copy(
-            src_ref=pack.at[source], dst_ref=circ_far.at[slot, gy],
-            send_sem=far_send.at[g], recv_sem=far_recv.at[slot, gy],
+            src_ref=pack.at[source, group], dst_ref=circ_far.at[slot, group, gy],
+            send_sem=far_send.at[group, g], recv_sem=far_recv.at[slot, group, gy],
             device_id=(other_end, g), device_id_type=MESH,
         )
 
-    def from_far(slot, g):
+    def from_far(slot, group, g):
         return pltpu.make_async_remote_copy(
-            src_ref=pack_lo.at[slot], dst_ref=circ_far.at[slot, g],
-            send_sem=far_send.at[g], recv_sem=far_recv.at[slot, g],
+            src_ref=pack_lo.at[slot, group], dst_ref=circ_far.at[slot, group, g],
+            send_sem=far_send.at[group, g], recv_sem=far_recv.at[slot, group, g],
             device_id=(other_end, g), device_id_type=MESH,
         )
 
     def to_near(pack, source, slot, i):
         return pltpu.make_async_remote_copy(
-            src_ref=pack.at[source, :, 0:3], dst_ref=circ_near.at[slot, gy],
+            src_ref=pack.at[source, 0], dst_ref=circ_near.at[slot, gy],
             send_sem=near_send.at[i], recv_sem=near_recv.at[slot, i],
             device_id=(gx, lax.rem(gy + i, gyn)), device_id_type=MESH,
         )
@@ -179,7 +181,7 @@
     def from_near(slot, i):
         sender = lax.rem(gy + gyn - i, gyn)
         return pltpu.make_async_remote_copy(
-            src_ref=pack_lo.at[slot, :, 0:3], dst_ref=circ_near.at[slot, sender],
+            src_ref=pack_lo.at[slot, 0], dst_ref=circ_near.at[slot, sender],
             send_sem=near_send.at[i], recv_sem=near_recv.at[slot, i],
             device_id=(gx, sender), device_id_type=MESH,
         )
@@ -196,15 +198,28 @@
             device_id=(above_gx, gy), device_id_type=MESH,
         )
 
-    def start_far(source, slot):
+    def at_ends(run):
         for end, pack in ((at_low, pack_lo), (at_high, pack_hi)):
 
             @pl.when(end)
             def _(pack=pack):
-                for g in range(gyn):
-                    to_far(pack, source, slot, g).start()
-                for i in range(1, gyn):
-                    to_near(pack, source, slot, i).start()
+                run(pack)
+
+    def start_far(source, slot):
+        def run(pack):
+            for g in range(gyn):
+                to_far(pack, source, slot, 0, g).start()
+
+        at_ends(run)
+
+    def start_ahead(source, slot):
+        def run(pack):
+            for i in range(1, gyn):
+                to_near(pack, source, slot, i).start()
+            for g in range(gyn):
+                to_far(pack, source, slot, 1, g).start()
+
+        at_ends(run)
 
     def start_rows(slot):
         @pl.when(not_low)
@@ -218,8 +233,9 @@
     def finish_sends(slot):
         @pl.when(at_end)
         def _():
-            for g in range(gyn):
-                to_far(pack_lo, slot, slot, g).wait_send()
+            for group in range(2):
+                for g in range(gyn):
+                    to_far(pack_lo, slot, slot, group, g).wait_send()
             for i in range(1, gyn):
                 to_near(pack_lo, slot, slot, i).wait_send()
 
@@ -255,6 +271,7 @@
     start_far(1, 0)
     to_west.start()
     to_east.start()
+    start_ahead(1, 0)
     to_west.wait()
     to_east.wait()
 
@@ -270,21 +287,21 @@
     def ghosts_of_neighbours(slot):
         @pl.when(not_high)
         def _():
-            outer = unpacked(load_pack(recv_hi, slot, (0, 1, 2)), 0)
-            inner = unpacked(load_pack(recv_hi, slot, (3, 4, 5)), 3)
+            outer = unpacked(load_pack(recv_hi, slot, 0), 0)
+            inner = unpacked(load_pack(recv_hi, slot, 1), 3)
             for f in range(7):
                 U[f, ABOVE] = jnp.where(rows8 < 3, outer[f], inner[f])
 
         @pl.when(not_low)
         def _():
-            outer = unpacked(load_pack(recv_lo, slot, (0, 1, 2)), 5)
-            inner = unpacked(load_pack(recv_lo, slot, (3, 4, 5)), 2)
+            outer = unpacked(load_pack(recv_lo, slot, 0), 5)
+            inner = unpacked(load_pack(recv_lo, slot, 1), 2)
             for f in range(7):
                 U[f, BELOW] = jnp.where(rows8 >= 5, outer[f], inner[f])
 
     wrapped = jnp.where(columns < 320, columns, columns - LANES)
 
-    def window(ring, parts, moved):
+    def window(ring, moved):
         origin = lax.rem(gy * 256 + moved + 512 * gyn, 256 * gyn)
         first_block = lax.div(origin, 256)
         offset = lax.rem(origin, 256)
@@ -302,7 +319,7 @@
             at = wrapped + ahead
             sources.append((place, picks, jnp.logical_and(at >= 0, at < 256)))
         out = []
-        for part in parts:
+        for part in range(3):
             spans = [
                 jnp.concatenate([pltpu.roll(ring[place, vector, part], turn, 1) for vector, turn in picks], axis=1)
                 for place, picks, _ in sources
@@ -328,29 +345,45 @@
         U[f, BELOW] = jnp.where(rows8 < 2, far_rows, U[f, BELOW])
 
     def ghosts_of_far_end(slot, n):
+        shift = shift_ref[n]
+        fraction = frac_ref[n]
+
+        @pl.when(at_end)
+        def _():
+            for g in range(gyn):
+                from_far(slot, 0, g).wait_recv()
+            ring_far[0] = circ_far[slot, 0]
+
+        @pl.when(at_low)
+        def _():
+            for f, raw in enumerate(unpacked(window(ring_far.at[0], -shift), 5)):
+                low_ghosts(f, raw, fraction)
+
+        @pl.when(at_high)
+        def _():
+            for f, raw in enumerate(unpacked(window(ring_far.at[0], shift), 0)):
+                high_ghosts(f, raw, fraction)
+
+    def rows_ahead(slot, n):
+        shift, shift_next = shift_ref[n], shift_ref[n + 1]
+        fraction = frac_ref[n]
+        left, right = AHEAD
+
         @pl.when(at_end)
         def _():
             for i in range(1, gyn):
                 from_near(slot, i).wait_recv()
             for g in range(gyn):
-                from_far(slot, g).wait_recv()
-            for place in range(gyn):
-                ring_far[place] = circ_far[slot, place]
-                ring_near[place] = circ_near[slot, place]
-
-        shift, shift_next = shift_ref[n], shift_ref[n + 1]
-        fraction = frac_ref[n]
-        A, B = (0, 1, 2), (3, 4, 5)
-        left, right = AHEAD
+                from_far(slot, 1, g).wait_recv()
+            ring_far[1] = circ_far[slot, 1]
+            ring_near[...] = circ_near[slot]
 
         @pl.when(at_low)
         def _():
-            ring_near[gy] = pack_lo[slot, :, 0:3]
-            for f, raw in enumerate(unpacked(window(ring_far, A, -shift), 5)):
-                low_ghosts(f, raw, fraction)
-            outer = window(ring_far, A, -shift_next)
-            inner = unpacked(window(ring_far, B, -shift_next), 2)
-            beyond = window(ring_near, A, shift - shift_next)
+            ring_near[gy] = pack_lo[slot, 0]
+            outer = window(ring_far.at[0], -shift_next)
+            inner = unpacked(window(ring_far.at[1], -shift_next), 2)
+            beyond = window(ring_near, shift - shift_next)
             rows_a = unpacked(outer, 5)
             ghost = unpacked([blended(x, fraction, 1) for x in beyond], 0)
             mirror = unpacked([blended(x, fraction, -1) for x in outer], 3)
@@ -361,12 +394,10 @@
 
         @pl.when(at_high)
         def _():
-            ring_near[gy] = pack_hi[slot, :, 0:3]
-            for f, raw in enumerate(unpacked(window(ring_far, A, shift), 0)):
-                high_ghosts(f, raw, fraction)
-            outer = window(ring_far, A, shift_next)
-            inner = unpacked(window(ring_far, B, shift_next), 3)
-            beyond = window(ring_near, A, shift_next - shift)
+            ring_near[gy] = pack_hi[slot, 0]
+            outer = window(ring_far.at[0], shift_next)
+            inner = unpacked(window(ring_far.at[1], shift_next), 3)
+            beyond = window(ring_near, shift_next - shift)
             rows_a = unpacked(outer, 0)
             ghost = unpacked([blended(x, fraction, -1) for x in beyond], 5)
             mirror = unpacked([blended(x, fraction, 1) for x in outer], 2)
@@ -500,18 +531,12 @@
     def cells_of(k, stride):
         return [PART[i, k] - (0.5 * stride) * row_after(FX[i, k], FX[i, following(k)]) for i in range(5)]
 
-    def advance(n, last):
+    def advance(n, last, ring):
         fraction = frac_ref[n]
 
         def tiles(run):
-            for k in range(RING):
+            for k in ring:
                 run(k)
-            if not last:
-
-                @pl.when(at_end)
-                def _():
-                    for k in AHEAD:
-                        run(k)
 
         stride = 0.5 * TIMESTEP
         tiles(initial_primitives)
@@ -534,42 +559,38 @@
 
         tiles(slopes)
         tiles(lambda k: second_order(k, TIMESTEP, last))
-        kept = range(OWN) if last else range(RING)
-
-        def mended(emf, remote_row, towards, ours):
-            remote = blended(remote_row, fraction, towards)
-            return jnp.where(jnp.logical_and(first_row, ours), 0.5 * (emf + remote), emf)
-
-        emfs = [corner(k) for k in range(RING)]
-        low_fix = mended(emfs[0], roll(emfs[BELOW], -1, 0), -1, at_low)
-        high_fix = mended(emfs[ABOVE], roll(emfs[ABOVE], -6, 0), 1, at_high)
-        emfs[0], emfs[ABOVE] = low_fix, high_fix
-        for k in range(RING):
-            new_bx = face_x(k, emfs[k], TIMESTEP)
-            if k in kept:
-                U[BX, k] = new_bx
-
         def new_cells(k):
             for field, value in zip((D, MX, MY, MZ, BZ), cells_of(k, TIMESTEP)):
                 U[field, k] = value
             U[BY, k] = face_y(k, TIMESTEP)
 
+        if ring == AHEAD:
+            left, right = AHEAD
+            emf_l, emf_r = corner(left), corner(right)
+            from_low = blended(roll(emf_r, -6, 0), fraction, 1)
+            from_high = blended(roll(emf_l, -2, 0), fraction, -1)
+            remote = jnp.where(at_low, from_low, from_high)
+            emf_r = jnp.where(first_row, 0.5 * (emf_r + remote), emf_r)
+            U[BX, left] = face_x(left, emf_l, TIMESTEP)
+            U[BX, right] = face_x(right, emf_r, TIMESTEP)
+            tiles(new_cells)
+            return
+        kept = range(OWN) if last else ring
+
+        def mended(emf, remote_row, towards, ours):
+            remote = blended(remote_row, fraction, towards)
+            return jnp.where(jnp.logical_and(first_row, ours), 0.5 * (emf + remote), emf)
+
+        emfs = [corner(k) for k in ring]
+        low_fix = mended(emfs[0], roll(emfs[BELOW], -1, 0), -1, at_low)
+        high_fix = mended(emfs[ABOVE], roll(emfs[ABOVE], -6, 0), 1, at_high)
+        emfs[0], emfs[ABOVE] = low_fix, high_fix
+        for k in ring:
+            new_bx = face_x(k, emfs[k], TIMESTEP)
+            if k in kept:
+                U[BX, k] = new_bx
         for k in kept:
             new_cells(k)
-        if not last:
-
-            @pl.when(at_end)
-            def _():
-                left, right = AHEAD
-                emf_l, emf_r = corner(left), corner(right)
-                from_low = blended(roll(emf_r, -6, 0), fraction, 1)
-                from_high = blended(roll(emf_l, -2, 0), fraction, -1)
-                remote = jnp.where(at_low, from_low, from_high)
-                emf_r = jnp.where(first_row, 0.5 * (emf_r + remote), emf_r)
-                U[BX, left] = face_x(left, emf_l, TIMESTEP)
-                U[BX, right] = face_x(right, emf_r, TIMESTEP)
-                for k in AHEAD:
-                    new_cells(k)
 
     rounds = STEPS // 2
 
@@ -586,9 +607,15 @@
 
         ghosts_of_neighbours(slot)
         ghosts_of_far_end(slot, 2 * r)
-        advance(2 * r, False)
+        advance(2 * r, False, MAIN)
+        rows_ahead(slot, 2 * r)
+
+        @pl.when(at_end)
+        def _():
+            advance(2 * r, False, AHEAD)
+
         ghosts_from_ahead(2 * r + 1)
-        advance(2 * r + 1, True)
+        advance(2 * r + 1, True, MAIN)
         finish_sends(slot)
 
         @pl.when(r < rounds - 1)
@@ -596,6 +623,7 @@
             pack_edges(1 - slot)
             start_far(1 - slot, 1 - slot)
             start_rows(1 - slot)
+            start_ahead(1 - slot, 1 - slot)
 
         return carry
 
@@ -619,12 +647,12 @@
     return [
         vmem(7, *tile), vmem(7, *tile), vmem(2, *tile), vmem(6, *tile), vmem(6, *tile), vmem(5, *tile), vmem(5, *tile),
         vmem(*tile), vmem(*tile), vmem(*tile), vmem(*tile), vmem(*tile),
-        *(vmem(2, 3, PARTS, 8, 128) for _ in range(4)), vmem(7, OWN, 8, 256),
-        vmem(2, gyn, 3, PARTS, 8, 128), vmem(2, gyn, 3, 3, 8, 128),
-        vmem(gyn, 3, PARTS, 8, 128), vmem(gyn, 3, 3, 8, 128), vmem(7, OWN, 8, 128), vmem(7, OWN, 8, 128),
+        *(vmem(2, GROUPS, 3, 3, 8, 128) for _ in range(4)), vmem(7, OWN, 8, 256),
+        vmem(2, GROUPS, gyn, 3, 3, 8, 128), vmem(2, gyn, 3, 3, 8, 128),
+        vmem(GROUPS, gyn, 3, 3, 8, 128), vmem(gyn, 3, 3, 8, 128), vmem(7, OWN, 8, 128), vmem(7, OWN, 8, 128),
         pltpu.SMEM((STEPS,), jnp.int32), pltpu.SMEM((STEPS,), f32), dma((5,)),
         dma((2,)), dma((2,)), dma((2,)), dma((2, 2)),
-        dma((gyn,)), dma((2, gyn)), dma((gyn,)), dma((2, gyn)),
+        dma((GROUPS, gyn)), dma((2, GROUPS, gyn)), dma((gyn,)), dma((2, gyn)),
     ]
 
 

time: 75.9 us -> 69.1 us (0.910)
  Pallas kernels: 69.9 us -> 62.9 us
    pallas_call x1, Pallas kernels: 69.9 us -> 62.9 us  [per_device(): pl.pallas_call(functools.partial(kernel, gxn, gyn), name='shearing_box',...]
where the time goes in v3:
time: 69.1 us; the launch traced here: 68.7 us
  Pallas kernels  62.9 us (91%)
  local copies, waits for them, and re-layouts  5.09 us (7%)
    pallas_call x1, Pallas kernels, per_device(): pl.pallas_call(functools.partial(kernel, gxn, gyn), name='shearing_box',...  62.9 us
    unnamed x13, local copies, waits for them, and re-layouts  5.09 us

profile of v3, /device:TPU:0, one launch (start us, length us, event | category | flops | bytes accessed | tf_op | source)
XLA Modules:
  0.0 68.7 jit_solution(13881461143512055803)
XLA Ops:
  0.6 0.0 copy-start.3
  0.6 0.0 copy-start.4
  0.7 0.6 copy-done.3
  1.3 0.0 copy-done.4
  1.3 0.0 copy-start
  1.3 0.9 %copy-done = f32[3,32,256]{2,1,0:T(8,128)S(1)} copy-done((f32[3,32,256]{2,1,0:T(8,128)S(1)}, f32[3,32,256]{2,1,0:T(8,128)}, u32[]{:S(2)}) %copy-start) | copy-done | bytes 98328
  2.2 0.0 copy-start.1
  2.2 0.9 %copy-done.1 = f32[3,32,256]{2,1,0:T(8,128)S(1)} copy-done((f32[3,32,256]{2,1,0:T(8,128)S(1)}, f32[3,32,256]{2,1,0:T(8,128)}, u32[]{:S(2)}) %copy-start.1) | copy-done | bytes 98328
  3.1 0.0 copy-start.2
  3.1 0.8 %copy-done.2 = f32[32,256]{1,0:T(8,128)S(1)} copy-done((f32[32,256]{1,0:T(8,128)S(1)}, f32[32,256]{1,0:T(8,128)}, u32[]{:S(2)}) %copy-start.2) | copy-done | bytes 32792
  3.8 62.9 %shearing_box.1 = (f32[32,256]{1,0:T(8,128)S(1)}, f32[3,32,256]{2,1,0:T(8,128)S(1)}, f32[3,32,256]{2,1,0:T(8,128)S(1)}) custom-call(s32[8]{0:T(128)S(1)} %copy-done.3, f32[8]{0:T(128)S(1)} %copy-done.4, f32[4,8,256]{2,1,0:T(8,128)S(1)} %bitcast.5, f32[3,4,8,256]{3,2,1,0:T(8,128)S(1)} %bitcast.3, f32[3,4,8,256]{3,2,1,0:T(8,128)S(1)} %bitcast.4), custom_call_target="tpu_custom_call" | custom-call | tf_op jit(solution)/shard_map/shearing_box/pallas_call | solution.py:663
  66.8 0.6 copy.11
  67.4 0.6 copy.12
  68.0 0.6 copy.13
Async XLA Ops:
  0.6 0.7 copy-start.3
  0.6 0.7 copy-start.4
  1.3 0.9 %copy-start = (f32[3,32,256]{2,1,0:T(8,128)S(1)}, f32[3,32,256]{2,1,0:T(8,128)}, u32[]{:S(2)}) copy-start(f32[3,32,256]{2,1,0:T(8,128)} %param.6) | copy-start | bytes 294916
  2.2 0.9 %copy-start.1 = (f32[3,32,256]{2,1,0:T(8,128)S(1)}, f32[3,32,256]{2,1,0:T(8,128)}, u32[]{:S(2)}) copy-start(f32[3,32,256]{2,1,0:T(8,128)} %param.7) | copy-start | bytes 294916
  3.1 0.8 %copy-start.2 = (f32[32,256]{1,0:T(8,128)S(1)}, f32[32,256]{1,0:T(8,128)}, u32[]{:S(2)}) copy-start(f32[32,256]{1,0:T(8,128)} %param.5) | copy-start | bytes 98308

commit v4 on v3

--- a/solution.py
+++ b/solution.py
@@ -40,7 +40,7 @@
 def kernel(
     gxn, gyn, shift_in, frac_in, den, mom, mag, den_out, mom_out, mag_out,
     U, Q, M, QL, QR, FX, PART, FY4, SX4, EZ, NBX, NBY,
-    pack_lo, pack_hi, recv_lo, recv_hi, block, circ_far, circ_near, ring_far, ring_near, col_r, col_l,
+    pack_lo, pack_hi, recv_lo, recv_hi, fold, block, circ_far, circ_near, ring_far, ring_near, col_r, col_l,
     shift_ref, frac_ref, load_sem,
     col_send, col_recv, row_send, row_recv, far_send, far_recv, near_send, near_recv,
 ):
@@ -143,8 +143,7 @@
             move(tiles[2], 0), move(tiles[2], 3), sixth,
         )
 
-    def pack_edge(ref, slot, k, outer, inner):
-        tiles = [U[f, k] for f in range(7)]
+    def pack_edge(ref, slot, tiles, outer, inner):
         for group, first in enumerate((outer, inner)):
             for part, tile in enumerate(packed(tiles, first)):
                 for lane in range(3):
@@ -153,27 +152,49 @@
     def load_pack(ref, slot, group):
         return [jnp.concatenate([ref[slot, group, lane, part] for lane in range(3)], axis=1) for part in range(3)]
 
-    def pack_edges(slot):
-        pack_edge(pack_lo, slot, 0, 0, 3)
-        pack_edge(pack_hi, slot, OWN - 1, 5, 2)
-
-    def to_far(pack, source, slot, group, g):
+    def pack_edges(slot, low_tiles, high_tiles):
+        pack_edge(pack_lo, slot, low_tiles, 0, 3)
+        pack_edge(pack_hi, slot, high_tiles, 5, 2)
+
+    def edges_of_block(slot):
+        pack_edges(slot, [U[f, 0] for f in range(7)], [U[f, OWN - 1] for f in range(7)])
+
+    lane = lane_iota((8, 128))
+
+    def at_ends(run):
+        for end, pack in ((at_low, pack_lo), (at_high, pack_hi)):
+
+            @pl.when(end)
+            def _(pack=pack):
+                run(pack)
+
+    def fold_edge(slot):
+        def run(pack):
+            for group in range(GROUPS):
+                for part in range(3):
+                    third = pack[slot, group, 2, part]
+                    fold[slot, group, 0, part] = jnp.where(lane < 86, pack[slot, group, 0, part], roll(third, 86, 1))
+                    fold[slot, group, 1, part] = jnp.where(lane < 85, pack[slot, group, 1, part], roll(third, 43, 1))
+
+        at_ends(run)
+
+    def to_far(slot, group, g):
         return pltpu.make_async_remote_copy(
-            src_ref=pack.at[source, group], dst_ref=circ_far.at[slot, group, gy],
+            src_ref=fold.at[slot, group], dst_ref=circ_far.at[slot, group, gy],
             send_sem=far_send.at[group, g], recv_sem=far_recv.at[slot, group, gy],
             device_id=(other_end, g), device_id_type=MESH,
         )
 
     def from_far(slot, group, g):
         return pltpu.make_async_remote_copy(
-            src_ref=pack_lo.at[slot, group], dst_ref=circ_far.at[slot, group, g],
+            src_ref=fold.at[slot, group], dst_ref=circ_far.at[slot, group, g],
             send_sem=far_send.at[group, g], recv_sem=far_recv.at[slot, group, g],
             device_id=(other_end, g), device_id_type=MESH,
         )
 
-    def to_near(pack, source, slot, i):
+    def to_near(slot, i):
         return pltpu.make_async_remote_copy(
-            src_ref=pack.at[source, 0], dst_ref=circ_near.at[slot, gy],
+            src_ref=fold.at[slot, 0], dst_ref=circ_near.at[slot, gy],
             send_sem=near_send.at[i], recv_sem=near_recv.at[slot, i],
             device_id=(gx, lax.rem(gy + i, gyn)), device_id_type=MESH,
         )
@@ -181,7 +202,7 @@
     def from_near(slot, i):
         sender = lax.rem(gy + gyn - i, gyn)
         return pltpu.make_async_remote_copy(
-            src_ref=pack_lo.at[slot, 0], dst_ref=circ_near.at[slot, sender],
+            src_ref=fold.at[slot, 0], dst_ref=circ_near.at[slot, sender],
             send_sem=near_send.at[i], recv_sem=near_recv.at[slot, i],
             device_id=(gx, sender), device_id_type=MESH,
         )
@@ -198,28 +219,19 @@
             device_id=(above_gx, gy), device_id_type=MESH,
         )
 
-    def at_ends(run):
-        for end, pack in ((at_low, pack_lo), (at_high, pack_hi)):
-
-            @pl.when(end)
-            def _(pack=pack):
-                run(pack)
-
-    def start_far(source, slot):
-        def run(pack):
+    def start_far(slot):
+        @pl.when(at_end)
+        def _():
             for g in range(gyn):
-                to_far(pack, source, slot, 0, g).start()
-
-        at_ends(run)
-
-    def start_ahead(source, slot):
-        def run(pack):
+                to_far(slot, 0, g).start()
+
+    def start_ahead(slot):
+        @pl.when(at_end)
+        def _():
             for i in range(1, gyn):
-                to_near(pack, source, slot, i).start()
+                to_near(slot, i).start()
             for g in range(gyn):
-                to_far(pack, source, slot, 1, g).start()
-
-        at_ends(run)
+                to_far(slot, 1, g).start()
 
     def start_rows(slot):
         @pl.when(not_low)
@@ -235,9 +247,9 @@
         def _():
             for group in range(2):
                 for g in range(gyn):
-                    to_far(pack_lo, slot, slot, group, g).wait_send()
+                    to_far(slot, group, g).wait_send()
             for i in range(1, gyn):
-                to_near(pack_lo, slot, slot, i).wait_send()
+                to_near(slot, i).wait_send()
 
         @pl.when(not_low)
         def _():
@@ -265,13 +277,14 @@
 
     own_columns = interleaved(block[...], 0, 256)
     U[:, 0:OWN] = own_columns
-    pack_edges(1)
+    edges_of_block(0)
+    fold_edge(0)
     pl.semaphore_wait(barrier, jnp.where(at_end, 2 * gyn, 4))
 
-    start_far(1, 0)
+    start_far(0)
     to_west.start()
     to_east.start()
-    start_ahead(1, 0)
+    start_ahead(0)
     to_west.wait()
     to_east.wait()
 
@@ -281,7 +294,7 @@
     for field in range(7):
         for k in (ABOVE, BELOW) + AHEAD:
             U[field, k] = U[field, 0]
-    pack_edges(0)
+    edges_of_block(0)
     start_rows(0)
 
     def ghosts_of_neighbours(slot):
@@ -311,20 +324,24 @@
             whole = lax.div(ahead + 2 * LANES, 3)
             phase = lax.rem(ahead + 2 * LANES, 3)
             place = lax.rem(first_block + i + gyn, gyn)
-            picks = []
+            turns = []
             for j in range(3):
-                vector = lax.rem(phase + j, 3)
-                turn = lax.rem(4 * 128 - whole - lax.div(phase + j, 3), 128)
-                picks.append((vector, turn))
+                turns.append(lax.rem(4 * 128 - whole - lax.div(phase + j, 3), 128))
             at = wrapped + ahead
-            sources.append((place, picks, jnp.logical_and(at >= 0, at < 256)))
+            sources.append((place, phase, turns, jnp.logical_and(at >= 0, at < 256)))
         out = []
         for part in range(3):
-            spans = [
-                jnp.concatenate([pltpu.roll(ring[place, vector, part], turn, 1) for vector, turn in picks], axis=1)
-                for place, picks, _ in sources
-            ]
-            out.append(jnp.where(sources[0][2], spans[0], jnp.where(sources[1][2], spans[1], spans[2])))
+            spans = []
+            for place, phase, turns, _ in sources:
+                one, two = ring[place, 0, part], ring[place, 1, part]
+                three = jnp.where(lane < 42, roll(one, -86, 1), roll(two, -43, 1))
+                vectors = (one, two, three)
+                picked = [
+                    jnp.where(phase == 0, vectors[j], jnp.where(phase == 1, vectors[(j + 1) % 3], vectors[(j + 2) % 3]))
+                    for j in range(3)
+                ]
+                spans.append(jnp.concatenate([pltpu.roll(x, turn, 1) for x, turn in zip(picked, turns)], axis=1))
+            out.append(jnp.where(sources[0][3], spans[0], jnp.where(sources[1][3], spans[1], spans[2])))
         return out
 
     def blended(x, fraction, towards):
@@ -380,7 +397,7 @@
 
         @pl.when(at_low)
         def _():
-            ring_near[gy] = pack_lo[slot, 0]
+            ring_near[gy] = fold[slot, 0]
             outer = window(ring_far.at[0], -shift_next)
             inner = unpacked(window(ring_far.at[1], -shift_next), 2)
             beyond = window(ring_near, shift - shift_next)
@@ -394,7 +411,7 @@
 
         @pl.when(at_high)
         def _():
-            ring_near[gy] = pack_hi[slot, 0]
+            ring_near[gy] = fold[slot, 0]
             outer = window(ring_far.at[0], shift_next)
             inner = unpacked(window(ring_far.at[1], shift_next), 3)
             beyond = window(ring_near, shift_next - shift)
@@ -531,7 +548,7 @@
     def cells_of(k, stride):
         return [PART[i, k] - (0.5 * stride) * row_after(FX[i, k], FX[i, following(k)]) for i in range(5)]
 
-    def advance(n, last, ring):
+    def advance(n, last, ring, ready_primitives=(), ready_fluxes=(), send_edges=None):
         fraction = frac_ref[n]
 
         def tiles(run):
@@ -539,8 +556,12 @@
                 run(k)
 
         stride = 0.5 * TIMESTEP
-        tiles(initial_primitives)
-        tiles(lambda k: first_order(k, stride))
+        for k in ring:
+            if k not in ready_primitives:
+                initial_primitives(k)
+        for k in ring:
+            if k not in ready_fluxes:
+                first_order(k, stride)
 
         def predicted_x(k):
             NBX[k] = face_x(k, corner(k), stride)
@@ -558,7 +579,8 @@
         tiles(predicted_cells)
 
         tiles(slopes)
-        tiles(lambda k: second_order(k, TIMESTEP, last))
+        if not last:
+            tiles(lambda k: second_order(k, TIMESTEP, False))
         def new_cells(k):
             for field, value in zip((D, MX, MY, MZ, BZ), cells_of(k, TIMESTEP)):
                 U[field, k] = value
@@ -581,14 +603,35 @@
             remote = blended(remote_row, fraction, towards)
             return jnp.where(jnp.logical_and(first_row, ours), 0.5 * (emf + remote), emf)
 
-        emfs = [corner(k) for k in ring]
-        low_fix = mended(emfs[0], roll(emfs[BELOW], -1, 0), -1, at_low)
-        high_fix = mended(emfs[ABOVE], roll(emfs[ABOVE], -6, 0), 1, at_high)
-        emfs[0], emfs[ABOVE] = low_fix, high_fix
+        def fixed_corners(ks):
+            emfs = {k: corner(k) for k in ks}
+            if 0 in ks:
+                emfs[0] = mended(emfs[0], roll(emfs[BELOW], -1, 0), -1, at_low)
+                emfs[ABOVE] = mended(emfs[ABOVE], roll(emfs[ABOVE], -6, 0), 1, at_high)
+            return emfs
+
+        if not last:
+            emfs = fixed_corners(ring)
+        else:
+            early, late = (0, OWN - 1, ABOVE, BELOW), range(1, OWN - 1)
+            for k in early:
+                second_order(k, TIMESTEP, True)
+            emfs = fixed_corners(early)
+            new_bx = {k: face_x(k, emfs[k], TIMESTEP) for k in early}
+
+            def edge_tiles(k):
+                density, mx, my, mz, bz = cells_of(k, TIMESTEP)
+                return [density, mx, my, mz, new_bx[k], face_y(k, TIMESTEP), bz]
+
+            send_edges(edge_tiles)
+            for k in late:
+                second_order(k, TIMESTEP, True)
+            emfs.update({k: corner(k) for k in (*late, OWN - 1)})
+        for k in kept:
+            U[BX, k] = face_x(k, emfs[k], TIMESTEP)
         for k in ring:
-            new_bx = face_x(k, emfs[k], TIMESTEP)
-            if k in kept:
-                U[BX, k] = new_bx
+            if k not in kept:
+                EZ[k] = emfs[k]
         for k in kept:
             new_cells(k)
 
@@ -597,6 +640,11 @@
     def two_steps(r, carry):
         slot = lax.rem(r, 2)
 
+        for k in range(OWN - 1):
+            initial_primitives(k)
+        for k in range(1, OWN - 1):
+            first_order(k, 0.5 * TIMESTEP)
+
         @pl.when(not_high)
         def _():
             down(slot).wait_recv()
@@ -607,7 +655,7 @@
 
         ghosts_of_neighbours(slot)
         ghosts_of_far_end(slot, 2 * r)
-        advance(2 * r, False, MAIN)
+        advance(2 * r, False, MAIN, tuple(range(OWN - 1)), tuple(range(1, OWN - 1)))
         rows_ahead(slot, 2 * r)
 
         @pl.when(at_end)
@@ -615,16 +663,18 @@
             advance(2 * r, False, AHEAD)
 
         ghosts_from_ahead(2 * r + 1)
-        advance(2 * r + 1, True, MAIN)
         finish_sends(slot)
 
-        @pl.when(r < rounds - 1)
-        def _():
-            pack_edges(1 - slot)
-            start_far(1 - slot, 1 - slot)
-            start_rows(1 - slot)
-            start_ahead(1 - slot, 1 - slot)
-
+        def send_edges(edge_tiles):
+            @pl.when(r < rounds - 1)
+            def _():
+                pack_edges(1 - slot, edge_tiles(0), edge_tiles(OWN - 1))
+                fold_edge(1 - slot)
+                start_far(1 - slot)
+                start_rows(1 - slot)
+                start_ahead(1 - slot)
+
+        advance(2 * r + 1, True, MAIN, send_edges=send_edges)
         return carry
 
     lax.fori_loop(0, rounds, two_steps, 0)
@@ -647,9 +697,9 @@
     return [
         vmem(7, *tile), vmem(7, *tile), vmem(2, *tile), vmem(6, *tile), vmem(6, *tile), vmem(5, *tile), vmem(5, *tile),
         vmem(*tile), vmem(*tile), vmem(*tile), vmem(*tile), vmem(*tile),
-        *(vmem(2, GROUPS, 3, 3, 8, 128) for _ in range(4)), vmem(7, OWN, 8, 256),
-        vmem(2, GROUPS, gyn, 3, 3, 8, 128), vmem(2, gyn, 3, 3, 8, 128),
-        vmem(GROUPS, gyn, 3, 3, 8, 128), vmem(gyn, 3, 3, 8, 128), vmem(7, OWN, 8, 128), vmem(7, OWN, 8, 128),
+        *(vmem(2, GROUPS, 3, 3, 8, 128) for _ in range(4)), vmem(2, GROUPS, 2, 3, 8, 128),
+        vmem(7, OWN, 8, 256), vmem(2, GROUPS, gyn, 2, 3, 8, 128), vmem(2, gyn, 2, 3, 8, 128),
+        vmem(GROUPS, gyn, 2, 3, 8, 128), vmem(gyn, 2, 3, 8, 128), vmem(7, OWN, 8, 128), vmem(7, OWN, 8, 128),
         pltpu.SMEM((STEPS,), jnp.int32), pltpu.SMEM((STEPS,), f32), dma((5,)),
         dma((2,)), dma((2,)), dma((2,)), dma((2, 2)),
         dma((GROUPS, gyn)), dma((2, GROUPS, gyn)), dma((gyn,)), dma((2, gyn)),

time: 69.1 us -> 62.2 us (0.900)
  Pallas kernels: 62.9 us -> 56.2 us
    pallas_call x1, Pallas kernels: 62.9 us -> 56.2 us  [per_device(): pl.pallas_call(functools.partial(kernel, gxn, gyn), name='shearing_box',...]
where the time goes in v4:
time: 62.2 us; the launch traced here: 61.9 us
  Pallas kernels  56.2 us (90%)
  local copies, waits for them, and re-layouts  5.09 us (8%)
  between operations  0.66 us (1%)
    pallas_call x1, Pallas kernels, per_device(): pl.pallas_call(functools.partial(kernel, gxn, gyn), name='shearing_box',...  56.2 us
    unnamed x13, local copies, waits for them, and re-layouts  5.09 us

profile of v4, /device:TPU:0, one launch (start us, length us, event | category | flops | bytes accessed | tf_op | source)
XLA Modules:
  0.0 61.9 jit_solution(14889317741047089797)
XLA Ops:
  0.6 0.0 copy-start.3
  0.6 0.0 copy-start.4
  0.7 0.6 %copy-done.3 = s32[8]{0:T(128)S(1)} copy-done((s32[8]{0:T(128)S(1)}, s32[8]{0:T(128)}, u32[]{:S(2)}) %copy-start.3) | copy-done | bytes 56
  1.3 0.0 copy-done.4
  1.3 0.0 copy-start
  1.3 0.9 %copy-done = f32[3,32,256]{2,1,0:T(8,128)S(1)} copy-done((f32[3,32,256]{2,1,0:T(8,128)S(1)}, f32[3,32,256]{2,1,0:T(8,128)}, u32[]{:S(2)}) %copy-start) | copy-done | bytes 98328
  2.2 0.0 copy-start.1
  2.2 0.9 %copy-done.1 = f32[3,32,256]{2,1,0:T(8,128)S(1)} copy-done((f32[3,32,256]{2,1,0:T(8,128)S(1)}, f32[3,32,256]{2,1,0:T(8,128)}, u32[]{:S(2)}) %copy-start.1) | copy-done | bytes 98328
  3.1 0.0 copy-start.2
  3.1 0.8 %copy-done.2 = f32[32,256]{1,0:T(8,128)S(1)} copy-done((f32[32,256]{1,0:T(8,128)S(1)}, f32[32,256]{1,0:T(8,128)}, u32[]{:S(2)}) %copy-start.2) | copy-done | bytes 32792
  3.8 56.2 %shearing_box.1 = (f32[32,256]{1,0:T(8,128)S(1)}, f32[3,32,256]{2,1,0:T(8,128)S(1)}, f32[3,32,256]{2,1,0:T(8,128)S(1)}) custom-call(s32[8]{0:T(128)S(1)} %copy-done.3, f32[8]{0:T(128)S(1)} %copy-done.4, f32[4,8,256]{2,1,0:T(8,128)S(1)} %bitcast.5, f32[3,4,8,256]{3,2,1,0:T(8,128)S(1)} %bitcast.3, f32[3,4,8,256]{3,2,1,0:T(8,128)S(1)} %bitcast.4), custom_call_target="tpu_custom_call" | custom-call | tf_op jit(solution)/shard_map/shearing_box/pallas_call | solution.py:713
  60.0 0.6 copy.11
  60.7 0.6 %copy.12 = f32[3,32,256]{2,1,0:T(8,128)} copy(f32[3,32,256]{2,1,0:T(8,128)S(1)} %get-tuple-element.7) | data formatting | bytes 196608
  61.3 0.6 %copy.13 = f32[3,32,256]{2,1,0:T(8,128)} copy(f32[3,32,256]{2,1,0:T(8,128)S(1)} %get-tuple-element.8) | data formatting | bytes 196608
Async XLA Ops:
  0.6 0.7 %copy-start.3 = (s32[8]{0:T(128)S(1)}, s32[8]{0:T(128)}, u32[]{:S(2)}) copy-start(s32[8]{0:T(128)} %shift_in.1) | copy-start | bytes 100
  0.6 0.7 %copy-start.4 = (f32[8]{0:T(128)S(1)}, f32[8]{0:T(128)}, u32[]{:S(2)}) copy-start(f32[8]{0:T(128)} %frac_in.1) | copy-start | bytes 100
  1.3 0.9 %copy-start = (f32[3,32,256]{2,1,0:T(8,128)S(1)}, f32[3,32,256]{2,1,0:T(8,128)}, u32[]{:S(2)}) copy-start(f32[3,32,256]{2,1,0:T(8,128)} %param.6) | copy-start | bytes 294916
  2.2 0.9 %copy-start.1 = (f32[3,32,256]{2,1,0:T(8,128)S(1)}, f32[3,32,256]{2,1,0:T(8,128)}, u32[]{:S(2)}) copy-start(f32[3,32,256]{2,1,0:T(8,128)} %param.7) | copy-start | bytes 294916
  3.1 0.8 %copy-start.2 = (f32[32,256]{1,0:T(8,128)S(1)}, f32[32,256]{1,0:T(8,128)}, u32[]{:S(2)}) copy-start(f32[32,256]{1,0:T(8,128)} %param.5) | copy-start | bytes 98308

commit v5 on v4

--- a/solution.py
+++ b/solution.py
@@ -56,6 +56,7 @@
     other_end = gxn - 1 - gx
     east = lax.rem(gy + 1, gyn)
     west = lax.rem(gy + gyn - 1, gyn)
+    far_order = sorted(range(gyn), key=lambda i: -min(i, gyn - i))
 
     rows8 = row_iota((8, LANES))
     first_row = rows8 == 0
@@ -102,8 +103,8 @@
 
     @pl.when(at_end)
     def _():
-        for g in range(gyn):
-            greet(other_end, g)
+        for i in far_order:
+            greet(other_end, lax.rem(gy + i, gyn))
         for i in range(1, gyn):
             greet(gx, lax.rem(gy + i, gyn))
 
@@ -178,11 +179,11 @@
 
         at_ends(run)
 
-    def to_far(slot, group, g):
+    def to_far(slot, group, i):
         return pltpu.make_async_remote_copy(
             src_ref=fold.at[slot, group], dst_ref=circ_far.at[slot, group, gy],
-            send_sem=far_send.at[group, g], recv_sem=far_recv.at[slot, group, gy],
-            device_id=(other_end, g), device_id_type=MESH,
+            send_sem=far_send.at[group, i], recv_sem=far_recv.at[slot, group, gy],
+            device_id=(other_end, lax.rem(gy + i, gyn)), device_id_type=MESH,
         )
 
     def from_far(slot, group, g):
@@ -222,16 +223,16 @@
     def start_far(slot):
         @pl.when(at_end)
         def _():
-            for g in range(gyn):
-                to_far(slot, 0, g).start()
+            for i in far_order:
+                to_far(slot, 0, i).start()
 
     def start_ahead(slot):
         @pl.when(at_end)
         def _():
             for i in range(1, gyn):
                 to_near(slot, i).start()
-            for g in range(gyn):
-                to_far(slot, 1, g).start()
+            for i in far_order:
+                to_far(slot, 1, i).start()
 
     def start_rows(slot):
         @pl.when(not_low)
@@ -689,6 +690,14 @@
     mag_out[...] = out[BX : BZ + 1]
 
 
+def store_kernel(den, mom, mag, den_out, mom_out, mag_out, sem):
+    copies = [pltpu.make_async_copy(a, b, sem.at[i]) for i, (a, b) in enumerate(((den, den_out), (mom, mom_out), (mag, mag_out)))]
+    for copy in copies:
+        copy.start()
+    for copy in copies:
+        copy.wait()
+
+
 def scratch(gyn):
     tile = (TILES, 8, LANES)
     f32 = jnp.float32
@@ -710,7 +719,7 @@
     gxn, gyn = mesh.shape["gx"], mesh.shape["gy"]
 
     def per_device(density, momentum, magnetic, shear_shift, shear_frac):
-        return pl.pallas_call(
+        state = pl.pallas_call(
             functools.partial(kernel, gxn, gyn),
             name="shearing_box",
             out_shape=tuple(jax.ShapeDtypeStruct(a.shape, jnp.float32) for a in (density, momentum, magnetic)),
@@ -727,6 +736,15 @@
             momentum.reshape(3, OWN, 8, 256),
             magnetic.reshape(3, OWN, 8, 256),
         )
+        return pl.pallas_call(
+            store_kernel,
+            name="store",
+            out_shape=tuple(jax.ShapeDtypeStruct(a.shape, jnp.float32) for a in (density, momentum, magnetic)),
+            in_specs=[pl.BlockSpec(memory_space=pltpu.VMEM)] * 3,
+            out_specs=tuple(pl.BlockSpec(memory_space=pl.ANY) for _ in range(3)),
+            scratch_shapes=[pltpu.SemaphoreType.DMA((3,))],
+            compiler_params=pltpu.CompilerParams(vmem_limit_bytes=48 * 1024 * 1024),
+        )(*state)
 
     return jax.shard_map(
         per_device,

time: 62.2 us -> 60.7 us (0.976)
  local copies, waits for them, and re-layouts: 5.09 us -> 3.2 us
    unnamed x13 -> x10, local copies, waits for them, and re-layouts: 5.09 us -> 3.2 us
    pallas_call x0 -> x1, Pallas kernels: none -> 0.71 us  [per_device(): pl.pallas_call(store_kernel, name='store', out_shape=tuple((jax.ShapeDtyp...]
where the time goes in v5:
time: 60.7 us; the launch traced here: 60.4 us
  Pallas kernels  56.6 us (93%)
  local copies, waits for them, and re-layouts  3.2 us (5%)
  between operations  0.66 us (1%)
    pallas_call x1, Pallas kernels, per_device(): pl.pallas_call(functools.partial(kernel, gxn, gyn), name='shearing_box',...  55.8 us
    unnamed x10, local copies, waits for them, and re-layouts  3.2 us

profile of v5, /device:TPU:0, one launch (start us, length us, event | category | flops | bytes accessed | tf_op | source)
XLA Modules:
  0.0 60.4 jit_solution(10599945831120950325)
XLA Ops:
  0.6 0.0 copy-start.3
  0.6 0.0 copy-start.4
  0.7 0.6 %copy-done.3 = s32[8]{0:T(128)S(1)} copy-done((s32[8]{0:T(128)S(1)}, s32[8]{0:T(128)}, u32[]{:S(2)}) %copy-start.3) | copy-done | bytes 56
  1.3 0.0 copy-done.4
  1.3 0.0 copy-start
  1.3 0.9 %copy-done = f32[3,32,256]{2,1,0:T(8,128)S(1)} copy-done((f32[3,32,256]{2,1,0:T(8,128)S(1)}, f32[3,32,256]{2,1,0:T(8,128)}, u32[]{:S(2)}) %copy-start) | copy-done | bytes 98328
  2.2 0.0 copy-start.1
  2.2 0.9 %copy-done.1 = f32[3,32,256]{2,1,0:T(8,128)S(1)} copy-done((f32[3,32,256]{2,1,0:T(8,128)S(1)}, f32[3,32,256]{2,1,0:T(8,128)}, u32[]{:S(2)}) %copy-start.1) | copy-done | bytes 98328
  3.1 0.0 copy-start.2
  3.1 0.8 %copy-done.2 = f32[32,256]{1,0:T(8,128)S(1)} copy-done((f32[32,256]{1,0:T(8,128)S(1)}, f32[32,256]{1,0:T(8,128)}, u32[]{:S(2)}) %copy-start.2) | copy-done | bytes 32792
  3.8 55.8 %shearing_box.1 = (f32[32,256]{1,0:T(8,128)S(1)}, f32[3,32,256]{2,1,0:T(8,128)S(1)}, f32[3,32,256]{2,1,0:T(8,128)S(1)}) custom-call(s32[8]{0:T(128)S(1)} %copy-done.3, f32[8]{0:T(128)S(1)} %copy-done.4, f32[4,8,256]{2,1,0:T(8,128)S(1)} %bitcast.5, f32[3,4,8,256]{3,2,1,0:T(8,128)S(1)} %bitcast.3, f32[3,4,8,256]{3,2,1,0:T(8,128)S(1)} %bitcast.4), custom_call_target="tpu_custom_call" | custom-call | tf_op jit(solution)/shard_map/shearing_box/pallas_call | solution.py:722
  59.7 0.7 %store.1 = (f32[32,256]{1,0:T(8,128)}, f32[3,32,256]{2,1,0:T(8,128)}, f32[3,32,256]{2,1,0:T(8,128)}) custom-call(f32[32,256]{1,0:T(8,128)S(1)} %get-tuple-element.6.den, f32[3,32,256]{2,1,0:T(8,128)S(1)} %get-tuple-element.7.mom, f32[3,32,256]{2,1,0:T(8,128)S(1)} %get-tuple-element.8.mag), custom_call_target="tpu_custom_call" | custom-call | tf_op jit(solution)/shard_map/store/pallas_call | solution.py:739
Async XLA Ops:
  0.6 0.7 %copy-start.3 = (s32[8]{0:T(128)S(1)}, s32[8]{0:T(128)}, u32[]{:S(2)}) copy-start(s32[8]{0:T(128)} %shift_in.1) | copy-start | bytes 100
  0.6 0.7 %copy-start.4 = (f32[8]{0:T(128)S(1)}, f32[8]{0:T(128)}, u32[]{:S(2)}) copy-start(f32[8]{0:T(128)} %frac_in.1) | copy-start | bytes 100
  1.3 0.9 %copy-start = (f32[3,32,256]{2,1,0:T(8,128)S(1)}, f32[3,32,256]{2,1,0:T(8,128)}, u32[]{:S(2)}) copy-start(f32[3,32,256]{2,1,0:T(8,128)} %param.6) | copy-start | bytes 294916
  2.2 0.9 %copy-start.1 = (f32[3,32,256]{2,1,0:T(8,128)S(1)}, f32[3,32,256]{2,1,0:T(8,128)}, u32[]{:S(2)}) copy-start(f32[3,32,256]{2,1,0:T(8,128)} %param.7) | copy-start | bytes 294916
  3.1 0.8 %copy-start.2 = (f32[32,256]{1,0:T(8,128)S(1)}, f32[32,256]{1,0:T(8,128)}, u32[]{:S(2)}) copy-start(f32[32,256]{1,0:T(8,128)} %param.5) | copy-start | bytes 98308

commit v6 on v5

--- a/solution.py
+++ b/solution.py
@@ -40,7 +40,7 @@
 def kernel(
     gxn, gyn, shift_in, frac_in, den, mom, mag, den_out, mom_out, mag_out,
     U, Q, M, QL, QR, FX, PART, FY4, SX4, EZ, NBX, NBY,
-    pack_lo, pack_hi, recv_lo, recv_hi, fold, block, circ_far, circ_near, ring_far, ring_near, col_r, col_l,
+    pack, recv, fold, block, circ_far, circ_near, ring_far, ring_near, col_out, col_r, col_l, halo_columns,
     shift_ref, frac_ref, load_sem,
     col_send, col_recv, row_send, row_recv, far_send, far_recv, near_send, near_recv,
 ):
@@ -49,6 +49,7 @@
     at_low = gx == 0
     at_high = gx == gxn - 1
     at_end = jnp.logical_or(at_low, at_high)
+    not_end = jnp.logical_not(at_end)
     not_low = gx > 0
     not_high = gx < gxn - 1
     below_gx = lax.max(gx - 1, 0)
@@ -134,50 +135,49 @@
             jnp.where(rows8 < 3, at(4, 0), at(5, 3)),
         ]
 
+    def turned_rows(x, amount):
+        return pltpu.roll(x, amount & 7, 0)
+
     def unpacked(tiles, first):
         def move(x, row):
-            return x if row == first else roll(x, first - row, 0)
-
-        sixth = jnp.where(((rows8 - first) & 7) < 2, move(tiles[0], 6), move(tiles[1], 4))
+            return turned_rows(x, first + 8 - row)
+
+        sixth = jnp.where(((rows8 + 8 - first) & 7) < 2, move(tiles[0], 6), move(tiles[1], 4))
         return (
             move(tiles[0], 0), move(tiles[0], 3), move(tiles[1], 0), move(tiles[1], 3),
             move(tiles[2], 0), move(tiles[2], 3), sixth,
         )
 
-    def pack_edge(ref, slot, tiles, outer, inner):
+    def by_end(low, high):
+        return jnp.where(at_low, low, high)
+
+    def pack_edge(side, slot, tiles, outer, inner):
         for group, first in enumerate((outer, inner)):
             for part, tile in enumerate(packed(tiles, first)):
                 for lane in range(3):
-                    ref[slot, group, lane, part] = tile[:, 128 * lane : 128 * (lane + 1)]
-
-    def load_pack(ref, slot, group):
-        return [jnp.concatenate([ref[slot, group, lane, part] for lane in range(3)], axis=1) for part in range(3)]
+                    pack[side, slot, group, lane, part] = tile[:, 128 * lane : 128 * (lane + 1)]
+
+    def load_pack(side, slot, group):
+        return [jnp.concatenate([recv[side, slot, group, lane, part] for lane in range(3)], axis=1) for part in range(3)]
 
     def pack_edges(slot, low_tiles, high_tiles):
-        pack_edge(pack_lo, slot, low_tiles, 0, 3)
-        pack_edge(pack_hi, slot, high_tiles, 5, 2)
+        pack_edge(0, slot, low_tiles, 0, 3)
+        pack_edge(1, slot, high_tiles, 5, 2)
 
     def edges_of_block(slot):
         pack_edges(slot, [U[f, 0] for f in range(7)], [U[f, OWN - 1] for f in range(7)])
 
     lane = lane_iota((8, 128))
 
-    def at_ends(run):
-        for end, pack in ((at_low, pack_lo), (at_high, pack_hi)):
-
-            @pl.when(end)
-            def _(pack=pack):
-                run(pack)
+    end_side = by_end(0, 1)
+    inner_side = 1 - end_side
 
     def fold_edge(slot):
-        def run(pack):
-            for group in range(GROUPS):
-                for part in range(3):
-                    third = pack[slot, group, 2, part]
-                    fold[slot, group, 0, part] = jnp.where(lane < 86, pack[slot, group, 0, part], roll(third, 86, 1))
-                    fold[slot, group, 1, part] = jnp.where(lane < 85, pack[slot, group, 1, part], roll(third, 43, 1))
-
-        at_ends(run)
+        for group in range(GROUPS):
+            for part in range(3):
+                first, second, third = (pack[end_side, slot, group, j, part] for j in range(3))
+                fold[slot, group, 0, part] = jnp.where(lane < 86, first, roll(third, 86, 1))
+                fold[slot, group, 1, part] = jnp.where(lane < 85, second, roll(third, 43, 1))
 
     def to_far(slot, group, i):
         return pltpu.make_async_remote_copy(
@@ -208,64 +208,62 @@
             device_id=(gx, sender), device_id_type=MESH,
         )
 
-    def down(slot):
+    def to_row(slot, side):
+        to_gx = jnp.where(side == 0, below_gx, above_gx)
         return pltpu.make_async_remote_copy(
-            src_ref=pack_lo.at[slot], dst_ref=recv_hi.at[slot], send_sem=row_send.at[0], recv_sem=row_recv.at[slot, 0],
-            device_id=(below_gx, gy), device_id_type=MESH,
-        )
-
-    def up(slot):
-        return pltpu.make_async_remote_copy(
-            src_ref=pack_hi.at[slot], dst_ref=recv_lo.at[slot], send_sem=row_send.at[1], recv_sem=row_recv.at[slot, 1],
-            device_id=(above_gx, gy), device_id_type=MESH,
-        )
-
-    def start_far(slot):
+            src_ref=pack.at[side, slot], dst_ref=recv.at[side, slot],
+            send_sem=row_send.at[side], recv_sem=row_recv.at[slot, side],
+            device_id=(to_gx, gy), device_id_type=MESH,
+        )
+
+    def start_exchange(slot, rows, between=lambda: None):
         @pl.when(at_end)
         def _():
+            fold_edge(slot)
             for i in far_order:
                 to_far(slot, 0, i).start()
-
-    def start_ahead(slot):
-        @pl.when(at_end)
-        def _():
+            if rows:
+                to_row(slot, inner_side).start()
+            between()
             for i in range(1, gyn):
                 to_near(slot, i).start()
             for i in far_order:
                 to_far(slot, 1, i).start()
 
-    def start_rows(slot):
-        @pl.when(not_low)
+        @pl.when(not_end)
         def _():
-            down(slot).start()
-
-        @pl.when(not_high)
+            if rows:
+                to_row(slot, 0).start()
+                to_row(slot, 1).start()
+            between()
+
+    def rows_arrived(slot):
+        to_row(slot, jnp.where(at_high, 1, 0)).wait_recv()
+
+        @pl.when(not_end)
         def _():
-            up(slot).start()
-
-    def finish_sends(slot):
-        @pl.when(at_end)
+            to_row(slot, 1).wait_recv()
+
+    def rows_sent(slot):
+        to_row(slot, jnp.where(at_low, 1, 0)).wait_send()
+
+        @pl.when(not_end)
         def _():
-            for group in range(2):
-                for g in range(gyn):
-                    to_far(slot, group, g).wait_send()
-            for i in range(1, gyn):
-                to_near(slot, i).wait_send()
-
-        @pl.when(not_low)
-        def _():
-            down(slot).wait_send()
-
-        @pl.when(not_high)
-        def _():
-            up(slot).wait_send()
+            to_row(slot, 1).wait_send()
+
+    def far_sent(slot):
+        for group in range(GROUPS):
+            for g in range(gyn):
+                to_far(slot, group, g).wait_send()
+        for i in range(1, gyn):
+            to_near(slot, i).wait_send()
 
     to_west = pltpu.make_async_remote_copy(
-        src_ref=block.at[:, :, :, 0:128], dst_ref=col_r, send_sem=col_send.at[0], recv_sem=col_recv.at[0],
+        src_ref=col_out.at[0], dst_ref=col_r, send_sem=col_send.at[0], recv_sem=col_recv.at[0],
         device_id=(gx, west), device_id_type=MESH,
     )
     to_east = pltpu.make_async_remote_copy(
-        src_ref=block.at[:, :, :, 128:256], dst_ref=col_l, send_sem=col_send.at[1], recv_sem=col_recv.at[1],
+        src_ref=col_out.at[1], dst_ref=col_l, send_sem=col_send.at[1], recv_sem=col_recv.at[1],
         device_id=(gx, east), device_id_type=MESH,
     )
 
@@ -278,40 +276,49 @@
 
     own_columns = interleaved(block[...], 0, 256)
     U[:, 0:OWN] = own_columns
+    near = lane < 64
+    for pair in range(4):
+        one, two = 2 * pair, min(2 * pair + 1, 6)
+        for k in range(OWN):
+            col_out[0, pair, k] = jnp.where(near, block[one, k, :, 0:128], roll(block[two, k, :, 0:128], 64, 1))
+            col_out[1, pair, k] = jnp.where(near, roll(block[one, k, :, 128:256], 64, 1), block[two, k, :, 128:256])
     edges_of_block(0)
-    fold_edge(0)
     pl.semaphore_wait(barrier, jnp.where(at_end, 2 * gyn, 4))
 
-    start_far(0)
-    to_west.start()
-    to_east.start()
-    start_ahead(0)
+    def start_columns():
+        to_west.start()
+        to_east.start()
+
+    start_exchange(0, False, start_columns)
     to_west.wait()
     to_east.wait()
 
-    near = lane_iota((7, OWN, 8, 128)) < 64
-    halo = interleaved(jnp.where(near, col_r[...], col_l[...]), 256, 384)
+    for field in range(7):
+        for k in range(OWN):
+            right, left = col_r[field // 2, k], col_l[field // 2, k]
+            if field % 2:
+                halo_columns[field, k] = jnp.where(near, roll(right, 64, 1), left)
+            else:
+                halo_columns[field, k] = jnp.where(near, right, roll(left, 64, 1))
+    halo = interleaved(halo_columns[...], 256, 384)
     U[:, 0:OWN] = U[:, 0:OWN] + halo
     for field in range(7):
         for k in (ABOVE, BELOW) + AHEAD:
             U[field, k] = U[field, 0]
     edges_of_block(0)
-    start_rows(0)
+    to_row(0, jnp.where(at_low, 1, 0)).start()
+
+    @pl.when(not_end)
+    def _():
+        to_row(0, 1).start()
+
 
     def ghosts_of_neighbours(slot):
-        @pl.when(not_high)
-        def _():
-            outer = unpacked(load_pack(recv_hi, slot, 0), 0)
-            inner = unpacked(load_pack(recv_hi, slot, 1), 3)
+        for side, k, outer_first, inner_first, mask in ((0, ABOVE, 0, 3, rows8 < 3), (1, BELOW, 5, 2, rows8 >= 5)):
+            outer = unpacked(load_pack(side, slot, 0), outer_first)
+            inner = unpacked(load_pack(side, slot, 1), inner_first)
             for f in range(7):
-                U[f, ABOVE] = jnp.where(rows8 < 3, outer[f], inner[f])
-
-        @pl.when(not_low)
-        def _():
-            outer = unpacked(load_pack(recv_lo, slot, 0), 5)
-            inner = unpacked(load_pack(recv_lo, slot, 1), 2)
-            for f in range(7):
-                U[f, BELOW] = jnp.where(rows8 >= 5, outer[f], inner[f])
+                U[f, k] = jnp.where(mask, outer[f], inner[f])
 
     wrapped = jnp.where(columns < 320, columns, columns - LANES)
 
@@ -348,94 +355,67 @@
     def blended(x, fraction, towards):
         return (1.0 - fraction) * x + fraction * (lane_after(x) if towards == 1 else lane_before(x))
 
-    def low_ghosts(f, raw, fraction):
-        ghost = blended(raw, fraction, -1)
-        far_rows = roll(raw, 1, 0)
-        own = roll(blended(U[f, 0], fraction, 1), 1, 0)
-        U[f, BELOW] = jnp.where(rows8 >= 5, ghost, jnp.where(first_row, far_rows, own))
-        U[f, ABOVE] = jnp.where(rows8 >= 6, far_rows, U[f, ABOVE])
-
-    def high_ghosts(f, raw, fraction):
-        ghost = blended(raw, fraction, 1)
-        far_rows = roll(raw, 6, 0)
-        own = roll(blended(U[f, OWN - 1], fraction, -1), -2, 0)
-        U[f, ABOVE] = jnp.where(rows8 < 3, ghost, jnp.where(rows8 < 6, own, far_rows))
-        U[f, BELOW] = jnp.where(rows8 < 2, far_rows, U[f, BELOW])
+    def blended_out(x, fraction):
+        return (1.0 - fraction) * x + fraction * by_end(lane_before(x), lane_after(x))
+
+    def blended_back(x, fraction):
+        return (1.0 - fraction) * x + fraction * by_end(lane_after(x), lane_before(x))
+
+    ghost_first = by_end(5, 0)
+    ghost_above = jnp.logical_and(at_high, rows8 < 3)
+    own_above = jnp.logical_and(at_high, jnp.logical_and(rows8 >= 3, rows8 < 6))
+    ghost_below = jnp.logical_and(at_low, rows8 >= 5)
+    own_below = jnp.logical_and(at_low, jnp.logical_and(rows8 >= 1, rows8 < 5))
+    far_below = rows8 < by_end(1, 2)
+
+    def end_ghosts(f, raw, fraction):
+        ghost = blended_out(raw, fraction)
+        far_rows = turned_rows(raw, by_end(1, 6))
+        own = turned_rows(blended_back(by_end(U[f, 0], U[f, OWN - 1]), fraction), by_end(1, 6))
+        U[f, ABOVE] = jnp.where(
+            ghost_above, ghost, jnp.where(own_above, own, jnp.where(rows8 >= 6, far_rows, U[f, ABOVE]))
+        )
+        U[f, BELOW] = jnp.where(
+            ghost_below, ghost, jnp.where(own_below, own, jnp.where(far_below, far_rows, U[f, BELOW]))
+        )
 
     def ghosts_of_far_end(slot, n):
+        for g in range(gyn):
+            from_far(slot, 0, g).wait_recv()
+        ring_far[0] = circ_far[slot, 0]
         shift = shift_ref[n]
-        fraction = frac_ref[n]
-
-        @pl.when(at_end)
-        def _():
-            for g in range(gyn):
-                from_far(slot, 0, g).wait_recv()
-            ring_far[0] = circ_far[slot, 0]
-
-        @pl.when(at_low)
-        def _():
-            for f, raw in enumerate(unpacked(window(ring_far.at[0], -shift), 5)):
-                low_ghosts(f, raw, fraction)
-
-        @pl.when(at_high)
-        def _():
-            for f, raw in enumerate(unpacked(window(ring_far.at[0], shift), 0)):
-                high_ghosts(f, raw, fraction)
+        for f, raw in enumerate(unpacked(window(ring_far.at[0], by_end(-shift, shift)), ghost_first)):
+            end_ghosts(f, raw, frac_ref[n])
 
     def rows_ahead(slot, n):
+        for i in range(1, gyn):
+            from_near(slot, i).wait_recv()
+        for g in range(gyn):
+            from_far(slot, 1, g).wait_recv()
+        ring_far[1] = circ_far[slot, 1]
+        ring_near[...] = circ_near[slot]
+        ring_near[gy] = fold[slot, 0]
         shift, shift_next = shift_ref[n], shift_ref[n + 1]
         fraction = frac_ref[n]
         left, right = AHEAD
-
-        @pl.when(at_end)
-        def _():
-            for i in range(1, gyn):
-                from_near(slot, i).wait_recv()
-            for g in range(gyn):
-                from_far(slot, 1, g).wait_recv()
-            ring_far[1] = circ_far[slot, 1]
-            ring_near[...] = circ_near[slot]
-
-        @pl.when(at_low)
-        def _():
-            ring_near[gy] = fold[slot, 0]
-            outer = window(ring_far.at[0], -shift_next)
-            inner = unpacked(window(ring_far.at[1], -shift_next), 2)
-            beyond = window(ring_near, shift - shift_next)
-            rows_a = unpacked(outer, 5)
-            ghost = unpacked([blended(x, fraction, 1) for x in beyond], 0)
-            mirror = unpacked([blended(x, fraction, -1) for x in outer], 3)
-            raw = unpacked(beyond, 6)
-            for f in range(7):
-                U[f, left] = jnp.where(first_row, raw[f], jnp.where(rows8 < 5, inner[f], rows_a[f]))
-                U[f, right] = jnp.where(rows8 < 3, ghost[f], jnp.where(rows8 < 6, mirror[f], raw[f]))
-
-        @pl.when(at_high)
-        def _():
-            ring_near[gy] = fold[slot, 0]
-            outer = window(ring_far.at[0], shift_next)
-            inner = unpacked(window(ring_far.at[1], shift_next), 3)
-            beyond = window(ring_near, shift_next - shift)
-            rows_a = unpacked(outer, 0)
-            ghost = unpacked([blended(x, fraction, -1) for x in beyond], 5)
-            mirror = unpacked([blended(x, fraction, 1) for x in outer], 2)
-            raw = unpacked(beyond, 7)
-            for f in range(7):
-                U[f, left] = jnp.where(rows8 < 2, raw[f], jnp.where(rows8 < 5, mirror[f], ghost[f]))
-                U[f, right] = jnp.where(rows8 < 3, rows_a[f], jnp.where(last_row, raw[f], inner[f]))
+        ahead = by_end(-shift_next, shift_next)
+        outer = window(ring_far.at[0], ahead)
+        beyond = window(ring_near, ahead + by_end(shift, -shift))
+        inner = unpacked(window(ring_far.at[1], ahead), by_end(2, 3))
+        rows_a = unpacked(outer, ghost_first)
+        ghost = unpacked([blended_back(x, fraction) for x in beyond], by_end(0, 5))
+        mirror = unpacked([blended_out(x, fraction) for x in outer], by_end(3, 2))
+        raw = unpacked(beyond, by_end(6, 7))
+        raw_left, raw_right = rows8 < by_end(1, 2), rows8 >= by_end(6, 7)
+        for f in range(7):
+            middle = jnp.where(rows8 < 5, by_end(inner[f], mirror[f]), by_end(rows_a[f], ghost[f]))
+            U[f, left] = jnp.where(raw_left, raw[f], middle)
+            middle = jnp.where(rows8 < 3, by_end(ghost[f], rows_a[f]), by_end(mirror[f], inner[f]))
+            U[f, right] = jnp.where(raw_right, raw[f], middle)
 
     def ghosts_from_ahead(n):
-        fraction = frac_ref[n]
-
-        @pl.when(at_low)
-        def _():
-            for f in range(7):
-                low_ghosts(f, U[f, AHEAD[0]], fraction)
-
-        @pl.when(at_high)
-        def _():
-            for f in range(7):
-                high_ghosts(f, U[f, AHEAD[1]], fraction)
+        for f in range(7):
+            end_ghosts(f, by_end(U[f, AHEAD[0]], U[f, AHEAD[1]]), frac_ref[n])
 
     def minmod(a, b):
         return jnp.maximum(jnp.minimum(a, b), 0.0) + jnp.minimum(jnp.maximum(a, b), 0.0)
@@ -646,34 +626,29 @@
         for k in range(1, OWN - 1):
             first_order(k, 0.5 * TIMESTEP)
 
-        @pl.when(not_high)
-        def _():
-            down(slot).wait_recv()
-
-        @pl.when(not_low)
-        def _():
-            up(slot).wait_recv()
-
+        rows_arrived(slot)
         ghosts_of_neighbours(slot)
-        ghosts_of_far_end(slot, 2 * r)
-        advance(2 * r, False, MAIN, tuple(range(OWN - 1)), tuple(range(1, OWN - 1)))
-        rows_ahead(slot, 2 * r)
 
         @pl.when(at_end)
         def _():
+            ghosts_of_far_end(slot, 2 * r)
+
+        advance(2 * r, False, MAIN, tuple(range(OWN - 1)), tuple(range(1, OWN - 1)))
+
+        @pl.when(at_end)
+        def _():
+            rows_ahead(slot, 2 * r)
             advance(2 * r, False, AHEAD)
-
-        ghosts_from_ahead(2 * r + 1)
-        finish_sends(slot)
+            ghosts_from_ahead(2 * r + 1)
+            far_sent(slot)
+
+        rows_sent(slot)
 
         def send_edges(edge_tiles):
             @pl.when(r < rounds - 1)
             def _():
                 pack_edges(1 - slot, edge_tiles(0), edge_tiles(OWN - 1))
-                fold_edge(1 - slot)
-                start_far(1 - slot)
-                start_rows(1 - slot)
-                start_ahead(1 - slot)
+                start_exchange(1 - slot, True)
 
         advance(2 * r + 1, True, MAIN, send_edges=send_edges)
         return carry
@@ -706,9 +681,9 @@
     return [
         vmem(7, *tile), vmem(7, *tile), vmem(2, *tile), vmem(6, *tile), vmem(6, *tile), vmem(5, *tile), vmem(5, *tile),
         vmem(*tile), vmem(*tile), vmem(*tile), vmem(*tile), vmem(*tile),
-        *(vmem(2, GROUPS, 3, 3, 8, 128) for _ in range(4)), vmem(2, GROUPS, 2, 3, 8, 128),
+        vmem(2, 2, GROUPS, 3, 3, 8, 128), vmem(2, 2, GROUPS, 3, 3, 8, 128), vmem(2, GROUPS, 2, 3, 8, 128),
         vmem(7, OWN, 8, 256), vmem(2, GROUPS, gyn, 2, 3, 8, 128), vmem(2, gyn, 2, 3, 8, 128),
-        vmem(GROUPS, gyn, 2, 3, 8, 128), vmem(gyn, 2, 3, 8, 128), vmem(7, OWN, 8, 128), vmem(7, OWN, 8, 128),
+        vmem(GROUPS, gyn, 2, 3, 8, 128), vmem(gyn, 2, 3, 8, 128), vmem(2, 4, OWN, 8, 128), vmem(4, OWN, 8, 128), vmem(4, OWN, 8, 128), vmem(7, OWN, 8, 128),
         pltpu.SMEM((STEPS,), jnp.int32), pltpu.SMEM((STEPS,), f32), dma((5,)),
         dma((2,)), dma((2,)), dma((2,)), dma((2, 2)),
         dma((GROUPS, gyn)), dma((2, GROUPS, gyn)), dma((gyn,)), dma((2, gyn)),

time: 60.7 us -> 59.2 us (0.975)
  Pallas kernels: 56.6 us -> 55.1 us
    pallas_call x1, Pallas kernels: 55.8 us -> 54.4 us  [per_device(): pl.pallas_call(functools.partial(kernel, gxn, gyn), name='shearing_box',...]
where the time goes in v6:
time: 59.2 us; the launch traced here: 59 us
  Pallas kernels  55.1 us (93%)
  local copies, waits for them, and re-layouts  3.2 us (5%)
  between operations  0.66 us (1%)
    pallas_call x1, Pallas kernels, per_device(): pl.pallas_call(functools.partial(kernel, gxn, gyn), name='shearing_box',...  54.4 us
    unnamed x10, local copies, waits for them, and re-layouts  3.2 us

profile of v6, /device:TPU:0, one launch (start us, length us, event | category | flops | bytes accessed | tf_op | source)
XLA Modules:
  0.0 59.0 jit_solution(7151504556338016123)
XLA Ops:
  0.6 0.0 copy-start.3
  0.6 0.0 copy-start.4
  0.7 0.6 %copy-done.3 = s32[8]{0:T(128)S(1)} copy-done((s32[8]{0:T(128)S(1)}, s32[8]{0:T(128)}, u32[]{:S(2)}) %copy-start.3) | copy-done | bytes 56
  1.3 0.0 copy-done.4
  1.3 0.0 copy-start
  1.3 0.9 %copy-done = f32[3,32,256]{2,1,0:T(8,128)S(1)} copy-done((f32[3,32,256]{2,1,0:T(8,128)S(1)}, f32[3,32,256]{2,1,0:T(8,128)}, u32[]{:S(2)}) %copy-start) | copy-done | bytes 98328
  2.2 0.0 copy-start.1
  2.2 0.9 %copy-done.1 = f32[3,32,256]{2,1,0:T(8,128)S(1)} copy-done((f32[3,32,256]{2,1,0:T(8,128)S(1)}, f32[3,32,256]{2,1,0:T(8,128)}, u32[]{:S(2)}) %copy-start.1) | copy-done | bytes 98328
  3.1 0.0 copy-start.2
  3.1 0.8 %copy-done.2 = f32[32,256]{1,0:T(8,128)S(1)} copy-done((f32[32,256]{1,0:T(8,128)S(1)}, f32[32,256]{1,0:T(8,128)}, u32[]{:S(2)}) %copy-start.2) | copy-done | bytes 32792
  3.8 54.4 %shearing_box.1 = (f32[32,256]{1,0:T(8,128)S(1)}, f32[3,32,256]{2,1,0:T(8,128)S(1)}, f32[3,32,256]{2,1,0:T(8,128)S(1)}) custom-call(s32[8]{0:T(128)S(1)} %copy-done.3, f32[8]{0:T(128)S(1)} %copy-done.4, f32[4,8,256]{2,1,0:T(8,128)S(1)} %bitcast.5, f32[3,4,8,256]{3,2,1,0:T(8,128)S(1)} %bitcast.3, f32[3,4,8,256]{3,2,1,0:T(8,128)S(1)} %bitcast.4), custom_call_target="tpu_custom_call" | custom-call | tf_op jit(solution)/shard_map/shearing_box/pallas_call | solution.py:697
  58.3 0.7 %store.1 = (f32[32,256]{1,0:T(8,128)}, f32[3,32,256]{2,1,0:T(8,128)}, f32[3,32,256]{2,1,0:T(8,128)}) custom-call(f32[32,256]{1,0:T(8,128)S(1)} %get-tuple-element.6.den, f32[3,32,256]{2,1,0:T(8,128)S(1)} %get-tuple-element.7.mom, f32[3,32,256]{2,1,0:T(8,128)S(1)} %get-tuple-element.8.mag), custom_call_target="tpu_custom_call" | custom-call | tf_op jit(solution)/shard_map/store/pallas_call | solution.py:714
Async XLA Ops:
  0.6 0.7 %copy-start.3 = (s32[8]{0:T(128)S(1)}, s32[8]{0:T(128)}, u32[]{:S(2)}) copy-start(s32[8]{0:T(128)} %shift_in.1) | copy-start | bytes 100
  0.6 0.7 %copy-start.4 = (f32[8]{0:T(128)S(1)}, f32[8]{0:T(128)}, u32[]{:S(2)}) copy-start(f32[8]{0:T(128)} %frac_in.1) | copy-start | bytes 100
  1.3 0.9 %copy-start = (f32[3,32,256]{2,1,0:T(8,128)S(1)}, f32[3,32,256]{2,1,0:T(8,128)}, u32[]{:S(2)}) copy-start(f32[3,32,256]{2,1,0:T(8,128)} %param.6) | copy-start | bytes 294916
  2.2 0.9 %copy-start.1 = (f32[3,32,256]{2,1,0:T(8,128)S(1)}, f32[3,32,256]{2,1,0:T(8,128)}, u32[]{:S(2)}) copy-start(f32[3,32,256]{2,1,0:T(8,128)} %param.7) | copy-start | bytes 294916
  3.1 0.8 %copy-start.2 = (f32[32,256]{1,0:T(8,128)S(1)}, f32[32,256]{1,0:T(8,128)}, u32[]{:S(2)}) copy-start(f32[32,256]{1,0:T(8,128)} %param.5) | copy-start | bytes 98308

commit v7 on v6

--- a/solution.py
+++ b/solution.py
@@ -267,11 +267,19 @@
         device_id=(gx, east), device_id_type=MESH,
     )
 
+    def permuted(x, one_hot, dim):
+        picks = one_hot.astype(jnp.bfloat16)
+        total = None
+        for _ in range(3):
+            term = x.astype(jnp.bfloat16)
+            x = x - term.astype(jnp.float32)
+            moved = lax.dot_general(term, picks, (((1,), (dim,)), ((), ())), preferred_element_type=jnp.float32)
+            total = moved if total is None else total + moved
+        return total
+
     def interleaved(x, start, stop):
         flat = x.reshape(7 * OWN * 8, stop - start)
-        out = jnp.dot(
-            flat, permutation[start:stop], precision=lax.Precision.HIGHEST, preferred_element_type=jnp.float32
-        )
+        out = permuted(flat, permutation[start:stop], 0)
         return out.reshape(7, OWN, 8, LANES)
 
     own_columns = interleaved(block[...], 0, 256)
@@ -656,10 +664,7 @@
     lax.fori_loop(0, rounds, two_steps, 0)
 
     flat = U[:, 0:OWN].reshape(7 * OWN * 8, LANES)
-    out = lax.dot_general(
-        flat, permutation[0:256], (((1,), (1,)), ((), ())),
-        precision=lax.Precision.HIGHEST, preferred_element_type=jnp.float32,
-    ).reshape(7, 8 * OWN, 256)
+    out = permuted(flat, permutation[0:256], 1).reshape(7, 8 * OWN, 256)
     den_out[...] = out[D]
     mom_out[...] = out[MX : MZ + 1]
     mag_out[...] = out[BX : BZ + 1]

time: 59.2 us -> 57.8 us (0.976)
  Pallas kernels: 55.1 us -> 53.7 us
    pallas_call x1, Pallas kernels: 54.4 us -> 53 us  [per_device(): pl.pallas_call(functools.partial(kernel, gxn, gyn), name='shearing_box',...]
where the time goes in v7:
time: 57.8 us; the launch traced here: 57.6 us
  Pallas kernels  53.7 us (93%)
  local copies, waits for them, and re-layouts  3.2 us (6%)
  between operations  0.66 us (1%)
    pallas_call x1, Pallas kernels, per_device(): pl.pallas_call(functools.partial(kernel, gxn, gyn), name='shearing_box',...  53 us
    unnamed x10, local copies, waits for them, and re-layouts  3.2 us

profile of v7, /device:TPU:0, one launch (start us, length us, event | category | flops | bytes accessed | tf_op | source)
XLA Modules:
  0.0 57.6 jit_solution(16923000572991437972)
XLA Ops:
  0.6 0.0 copy-start.3
  0.6 0.0 copy-start.4
  0.7 0.6 %copy-done.3 = s32[8]{0:T(128)S(1)} copy-done((s32[8]{0:T(128)S(1)}, s32[8]{0:T(128)}, u32[]{:S(2)}) %copy-start.3) | copy-done | bytes 56
  1.3 0.0 copy-done.4
  1.3 0.0 copy-start
  1.3 0.9 %copy-done = f32[3,32,256]{2,1,0:T(8,128)S(1)} copy-done((f32[3,32,256]{2,1,0:T(8,128)S(1)}, f32[3,32,256]{2,1,0:T(8,128)}, u32[]{:S(2)}) %copy-start) | copy-done | bytes 98328
  2.2 0.0 copy-start.1
  2.2 0.9 %copy-done.1 = f32[3,32,256]{2,1,0:T(8,128)S(1)} copy-done((f32[3,32,256]{2,1,0:T(8,128)S(1)}, f32[3,32,256]{2,1,0:T(8,128)}, u32[]{:S(2)}) %copy-start.1) | copy-done | bytes 98328
  3.1 0.0 copy-start.2
  3.1 0.8 %copy-done.2 = f32[32,256]{1,0:T(8,128)S(1)} copy-done((f32[32,256]{1,0:T(8,128)S(1)}, f32[32,256]{1,0:T(8,128)}, u32[]{:S(2)}) %copy-start.2) | copy-done | bytes 32792
  3.8 53.0 %shearing_box.1 = (f32[32,256]{1,0:T(8,128)S(1)}, f32[3,32,256]{2,1,0:T(8,128)S(1)}, f32[3,32,256]{2,1,0:T(8,128)S(1)}) custom-call(s32[8]{0:T(128)S(1)} %copy-done.3, f32[8]{0:T(128)S(1)} %copy-done.4, f32[4,8,256]{2,1,0:T(8,128)S(1)} %bitcast.5, f32[3,4,8,256]{3,2,1,0:T(8,128)S(1)} %bitcast.3, f32[3,4,8,256]{3,2,1,0:T(8,128)S(1)} %bitcast.4), custom_call_target="tpu_custom_call" | custom-call | tf_op jit(solution)/shard_map/shearing_box/pallas_call | solution.py:702
  56.9 0.7 %store.1 = (f32[32,256]{1,0:T(8,128)}, f32[3,32,256]{2,1,0:T(8,128)}, f32[3,32,256]{2,1,0:T(8,128)}) custom-call(f32[32,256]{1,0:T(8,128)S(1)} %get-tuple-element.6.den, f32[3,32,256]{2,1,0:T(8,128)S(1)} %get-tuple-element.7.mom, f32[3,32,256]{2,1,0:T(8,128)S(1)} %get-tuple-element.8.mag), custom_call_target="tpu_custom_call" | custom-call | tf_op jit(solution)/shard_map/store/pallas_call | solution.py:719
Async XLA Ops:
  0.6 0.7 %copy-start.3 = (s32[8]{0:T(128)S(1)}, s32[8]{0:T(128)}, u32[]{:S(2)}) copy-start(s32[8]{0:T(128)} %shift_in.1) | copy-start | bytes 100
  0.6 0.7 %copy-start.4 = (f32[8]{0:T(128)S(1)}, f32[8]{0:T(128)}, u32[]{:S(2)}) copy-start(f32[8]{0:T(128)} %frac_in.1) | copy-start | bytes 100
  1.3 0.9 %copy-start = (f32[3,32,256]{2,1,0:T(8,128)S(1)}, f32[3,32,256]{2,1,0:T(8,128)}, u32[]{:S(2)}) copy-start(f32[3,32,256]{2,1,0:T(8,128)} %param.6) | copy-start | bytes 294916
  2.2 0.9 %copy-start.1 = (f32[3,32,256]{2,1,0:T(8,128)S(1)}, f32[3,32,256]{2,1,0:T(8,128)}, u32[]{:S(2)}) copy-start(f32[3,32,256]{2,1,0:T(8,128)} %param.7) | copy-start | bytes 294916
  3.1 0.8 %copy-start.2 = (f32[32,256]{1,0:T(8,128)S(1)}, f32[32,256]{1,0:T(8,128)}, u32[]{:S(2)}) copy-start(f32[32,256]{1,0:T(8,128)} %param.5) | copy-start | bytes 98308
